TPU v7x, 128 devices: a whole 4x4x4 slice. The times are simulated.
128 devices in a mesh: mem: 8 (over y, core), tile: 16 (over z, x).
Axes of the slice: x: 4, y: 4, z: 4, core: 2. Of those that a mesh axis runs over, the one named last changes fastest.
Arguments:
- solution: float32 [40, 4, 128, 1440], P('mem', None, 'tile'), may hold values from -6 to 6
- residual: float32 [40, 4, 128, 1440], P('mem', None, 'tile')
- direction: float32 [40, 4, 128, 1440], P('mem', None, 'tile')
- ensemble: bfloat16 [40, 4, 128, 1440], P('mem', None, 'tile'), may hold values from -6 to 6
- east_rate: float32 [128, 1440], P('tile'), may hold values from 0.06 to 0.12
- north_rate: float32 [128, 1440], P('tile'), may hold values from 0.18 to 0.36
- sea_mask: int32 [128, 1440], P('tile'), may hold values 0 or 1
- pass_counts: int32 [4], replicated, may hold values from 1 to 4, as said below
- obs_owner: int32 [131072, 1], P(('mem', 'tile')), may hold values from 0 to 127; in each aligned block of 1024 rows (0 to 1023, 1024 to 2047, ...) at most 16 rows name the same one
- obs_cell: int32 [131072], P(('mem', 'tile')), may hold values from 0 to 1439
- obs_level: int32 [131072], P(('mem', 'tile')), may hold values from 0 to 1
- obs_variable: int32 [131072], P(('mem', 'tile')), may hold values from 0 to 1
- obs_error: float32 [131072], P(('mem', 'tile')), may hold values from 0.5 to 2
Outputs:
- updated_solution: float32 [40, 4, 128, 1440], P('mem', None, 'tile')
- updated_residual: float32 [40, 4, 128, 1440], P('mem', None, 'tile')
Inputs may be any that keep to these rules, and one draw needn't show every extreme that they name: `pass_counts`: each field takes 1 to 4 passes; some field takes 4 and some field takes 1. `obs_owner`: owners are numbered d = (index along mem) * 16 + (index along tile) of the block of rows and longitudes they hold; the observations of one track segment name one owner at most 16 times, a bound that some block reaches. `obs_cell`: row within the band times 180 plus longitude within the block.
All inputs are finite; a program needn't handle non-finite values. No bound on the sum of `sea_mask` on one device may be relied on, other than what follows from the above.
Results may differ from a plain program's by a relative error of at most 0.0011.
Values may be sent and summed in bfloat16 or wider, within the bound.
A program may use at most 128 MiB of HBM per device.

v0:
```python
import math

import jax
import jax.numpy as jnp
from jax import lax
from jax.sharding import PartitionSpec as P

LEVELS = 2
PASSES = 4
ITERS = 2


CORRELATION = 0.6


def with_halo(block, sides, width):
    for axis, dim in sides:
        count = lax.axis_size(axis)
        forward = [(i, i + 1) for i in range(count - 1)]
        backward = [(target, source) for source, target in forward]
        low = lax.ppermute(
            lax.slice_in_dim(block, block.shape[dim] - width, None, axis=dim), axis, forward
        )
        high = lax.ppermute(lax.slice_in_dim(block, 0, width, axis=dim), axis, backward)
        block = jnp.concatenate([low, block, high], axis=dim)
    return block


def flow_step(padded, east_faces, north_faces):
    flux_north = north_faces * (padded[..., 1:, :] - padded[..., :-1, :])
    inner = padded[..., 1:-1, :]
    flux_east = east_faces * (jnp.roll(inner, -1, -1) - inner)
    return (
        inner
        + flux_east
        - jnp.roll(flux_east, 1, -1)
        + flux_north[..., 1:, :]
        - flux_north[..., :-1, :]
    )


def coefficients(east_rate, north_rate, sea_mask):
    margin = 1
    stacked = jnp.stack([east_rate, north_rate, sea_mask.astype(jnp.float32)])
    extended = with_halo(stacked, (("tile", 1),), margin)
    east_ext, north_ext, sea_ext = (extended[0], extended[1], extended[2])
    east_all = east_ext * sea_ext * jnp.roll(sea_ext, -1, 1)
    north_all = north_ext[:-1] * sea_ext[:-1] * sea_ext[1:]
    return (east_all, north_all, sea_ext, margin)


def smooth(field, coeffs, pass_counts):
    east_all, north_all, sea_ext, margin = coeffs
    band_rows = field.shape[2]
    sea_rows = sea_ext[margin : margin + band_rows]
    active = field * sea_rows
    applies = pass_counts[:, None, None]
    east_faces = east_all[margin : margin + band_rows]
    for sweep in range(PASSES):
        padded = with_halo(active, (("tile", 2),), 1)
        moved = flow_step(padded, east_faces, north_all)
        active = jnp.where(sweep < applies, moved, active)
    return active * sea_rows


def precision_apply(values, errors):
    scaled = values / errors
    length = scaled.shape[0]
    zero_col = jnp.zeros((1,), jnp.float32)
    following = jnp.concatenate([scaled[1:], zero_col])
    preceding = jnp.concatenate([zero_col, scaled[:-1]])
    position = jnp.arange(length, dtype=jnp.int32)
    at_ends = ((position == 0) | (position == length - 1)).astype(jnp.float32)
    diagonal = 1.0 + CORRELATION * CORRELATION - CORRELATION * CORRELATION * at_ends
    mixed = (diagonal * scaled - CORRELATION * (following + preceding)) / (
        1.0 - CORRELATION * CORRELATION
    )
    return mixed / errors


def shards(
    solution,
    residual,
    direction,
    ensemble,
    east_rate,
    north_rate,
    sea_mask,
    pass_counts,
    obs_owner,
    obs_cell,
    obs_level,
    obs_variable,
    obs_error,
):
    coeffs = coefficients(east_rate, north_rate, sea_mask)
    mem_count = lax.axis_size("mem")
    devices = mem_count * lax.axis_size("tile")
    weight = 1.0 / math.sqrt(ensemble.shape[0] * mem_count - 1)
    band_rows = solution.shape[2]
    block_cols = solution.shape[3] // mem_count
    owners = obs_owner[:, 0]
    segment = owners.shape[0]
    capacity = 2 * segment // devices
    one_hot = (owners[:, None] == jnp.arange(devices, dtype=jnp.int32)[None, :]).astype(jnp.int32)
    slot_index = jnp.sum(one_hot * (jnp.cumsum(one_hot, 0) - 1), 1)
    cell_index = (obs_variable * LEVELS + obs_level) * (band_rows * block_cols) + obs_cell
    send_ids = jnp.zeros((devices, capacity), jnp.int32).at[owners, slot_index].set(cell_index)
    wanted = lax.all_to_all(
        send_ids, ("mem", "tile"), split_axis=0, concat_axis=0, tiled=True
    ).reshape(-1)
    tiled_pert = lax.all_to_all(ensemble, "mem", split_axis=3, concat_axis=0, tiled=True)

    def global_sum(value):
        return lax.psum(value, ("mem", "tile"))

    norm_now = global_sum(jnp.sum(residual * residual))
    for iteration in range(ITERS):
        shaped = smooth(direction, coeffs, pass_counts).astype(jnp.bfloat16)
        gathered = lax.all_to_all(shaped, "mem", split_axis=3, concat_axis=0, tiled=True)
        increment = (
            jnp.sum(tiled_pert.astype(jnp.float32) * gathered.astype(jnp.float32), 0) * weight
        )
        picked = increment.reshape(-1)[wanted].reshape(devices, capacity)
        returned = lax.all_to_all(picked, ("mem", "tile"), split_axis=0, concat_axis=0, tiled=True)
        obs_value = returned[owners, slot_index]
        weighted = precision_apply(obs_value, obs_error)
        outgoing = jnp.zeros((devices, capacity), jnp.float32).at[owners, slot_index].set(weighted)
        arrived = lax.all_to_all(outgoing, ("mem", "tile"), split_axis=0, concat_axis=0, tiled=True)
        adjoint = (
            jnp.zeros((increment.size,), jnp.float32)
            .at[wanted]
            .add(arrived.reshape(-1))
            .reshape(increment.shape)
        )
        spread = (tiled_pert.astype(jnp.float32) * adjoint[None] * weight).astype(jnp.bfloat16)
        back = lax.all_to_all(spread, "mem", split_axis=0, concat_axis=3, tiled=True)
        image = direction + smooth(back.astype(jnp.float32), coeffs, pass_counts)
        step_size = norm_now / global_sum(jnp.sum(direction * image))
        solution = solution + step_size * direction
        residual = residual - step_size * image
        if iteration + 1 < ITERS:
            norm_next = global_sum(jnp.sum(residual * residual))
            direction = residual + norm_next / norm_now * direction
            norm_now = norm_next
    return (solution, residual)


def solution(mesh):
    return jax.shard_map(
        shards,
        mesh=mesh,
        in_specs=(
            P("mem", None, "tile", None),
            P("mem", None, "tile", None),
            P("mem", None, "tile", None),
            P("mem", None, "tile", None),
            P("tile", None),
            P("tile", None),
            P("tile", None),
            P(),
            P(("mem", "tile"), None),
            P(("mem", "tile")),
            P(("mem", "tile")),
            P(("mem", "tile")),
            P(("mem", "tile")),
        ),
        out_specs=(P("mem", None, "tile", None), P("mem", None, "tile", None)),
        check_vma=False,
    )
```

profile of v0, /device:TPU:1, one launch (start us, length us, event | category | flops | bytes accessed | tf_op | source)
XLA Modules:
  0.0 770.2 jit_solution(7420119793603275000)
XLA Ops:
  7.8 11.5 %all-to-all-start.1 = ((s32[128,1,16]{2,1,0:T(1,128)}), s32[128,1,16]{2,1,0:T(1,128)S(1)}, u32[]{:S(2)}, u32[]{:S(2)}) async-start(s32[128,1,16]{2,1,0:T(1,128)} %copy.101), calls=%async_computation.1 | async-start | bytes 131072 | tf_op jit(solution)/shard_map/all_to_all | solution.py:109
  33.4 16.8 %copy.96 = bf16[5,4,8,1440]{2,0,1,3:T(8,128)(2,1)} copy(bf16[5,4,8,1440]{3,2,1,0:T(8,128)(2,1)S(1)} %copy-done.10) | data formatting | bytes 921600 | tf_op args[3]
  50.2 11.8 %reshape.273 = bf16[8,2,14400]{2,1,0:T(2,128)(2,1)} reshape(bf16[1440,4,5,8]{3,2,1,0:T(8,128)(2,1)} %bitcast.97) | data formatting | bytes 921600
  110.3 10.5 %reshape.275 = bf16[8,2,14400]{2,1,0:T(2,128)(2,1)} reshape(bf16[1440,5,4,8]{3,2,1,0:T(4,128)(2,1)} %bitcast.98) | data formatting | bytes 921600
  127.8 10.9 %reshape.274 = bf16[1440,4,5,8]{3,2,1,0:T(8,128)(2,1)} reshape(bf16[8,2,14400]{2,1,0:T(2,128)(2,1)} %all-to-all-done) | data formatting | bytes 921600
  138.7 10.8 %copy.97 = bf16[5,4,8,1440]{3,2,1,0:T(8,128)(2,1)S(1)} copy(bf16[5,4,8,1440]{2,0,1,3:T(8,128)(2,1)} %bitcast.96) | data formatting | bytes 921600 | tf_op jit(solution)/shard_map/all_to_all | solution.py:112
  149.5 7.5 reshape.276
  157.0 8.6 %copy.103 = bf16[5,4,8,1440]{3,2,1,0:T(8,128)(2,1)S(1)} copy(bf16[5,4,8,1440]{2,1,0,3:T(4,128)(2,1)} %bitcast.99) | data formatting | bytes 921600 | tf_op jit(solution)/shard_map/all_to_all | solution.py:120
  171.2 11.8 %gather_fusion = f32[2048]{0:T(1024)S(1)} fusion(f32[5760]{0:T(1024)S(1)} %mul.420, s32[2048]{0:T(1024)S(1)} %broadcast_clamp_fusion), kind=kCustom, calls=%fused_computation | custom fusion | bytes 24576 | tf_op jit(solution)/shard_map/gather | solution.py:124
  183.1 28.9 %all_to_all.96 = f32[128,1,16]{2,1,0:T(1,128)S(1)} all-to-all(f32[128,1,16]{2,1,0:T(1,128)S(1)} %bitcast.128), channel_id=1, replica_groups=mesh['mem'=8,'tile'=16] {'mem','tile'}, dimensions={0} | all-to-all | bytes 16384 | tf_op jit(solution)/shard_map/all_to_all | solution.py:125
  241.9 11.4 %scatter_custom_fusion = f32[5760]{0:T(1024)S(1)} fusion(s32[2048]{0:T(1024)} %bitcast.136, f32[2048]{0:T(1024)S(1)} %reshape.208, f32[]{:T(128)} %constant.17.clone.1), kind=kCustom, calls=%fused_computation.204 | custom fusion | flops 2048 | bytes 23552 | tf_op jit(solution)/shard_map/scatter-add | solution.py:133
  260.3 10.0 %all-to-all-done.5 = bf16[40,4,8,180]{3,2,1,0:T(8,128)(2,1)} async-done(((bf16[40,4,8,180]{3,2,1,0:T(8,128)(2,1)}), bf16[40,4,8,180]{3,2,1,0:T(8,128)(2,1)}, u32[]{:S(2)}, u32[]{:S(2)}) %all-to-all-start.5) | async-done | bytes 460832 | tf_op jit(solution)/shard_map/all_to_all | solution.py:137
  313.3 77.9 %all-reduce = (f32[]{:T(128)}, f32[]{:T(128)}) all-reduce(f32[]{:T(128)} %multiply_reduce_fusion.5, f32[]{:T(128)} %get-tuple-element.10), channel_id=1, replica_groups=mesh['mem'=8,'tile'=16] {'mem','tile'}, use_global_device_ids=true, to_apply=%region_1.2 | all-reduce | flops 2 | bytes 16 | tf_op jit(solution)/shard_map/psum | solution.py:115
  394.9 63.8 %psum.30 = f32[]{:T(128)} all-reduce(f32[]{:T(128)} %get-tuple-element.8), channel_id=1, replica_groups=mesh['mem'=8,'tile'=16] {'mem','tile'}, use_global_device_ids=true, to_apply=%region_13.14 | all-reduce | flops 1 | bytes 8 | tf_op jit(solution)/shard_map/psum | solution.py:115
  498.0 8.8 %copy.109 = bf16[5,4,8,1440]{2,1,0,3:T(4,128)(2,1)} copy(bf16[5,4,8,1440]{3,2,1,0:T(8,128)(2,1)} %fusion.28) | data formatting | bytes 921600 | tf_op jit(solution)/shard_map/convert_element_type | solution.py:119
  506.7 9.8 %reshape.277 = bf16[8,2,14400]{2,1,0:T(2,128)(2,1)S(1)} reshape(bf16[1440,5,4,8]{3,2,1,0:T(4,128)(2,1)} %bitcast.100) | data formatting | bytes 921600
  516.5 16.8 %all_to_all.97 = bf16[8,2,14400]{2,1,0:T(2,128)(2,1)S(1)} all-to-all(bf16[8,2,14400]{2,1,0:T(2,128)(2,1)S(1)} %reshape.277), channel_id=1, replica_groups=mesh['mem'=8,'tile'=16] {'mem'}, dimensions={0} | all-to-all | bytes 921600 | tf_op jit(solution)/shard_map/all_to_all | solution.py:120
  540.8 8.6 %copy.110 = bf16[5,4,8,1440]{3,2,1,0:T(8,128)(2,1)S(1)} copy(bf16[5,4,8,1440]{2,1,0,3:T(4,128)(2,1)} %bitcast.101) | data formatting | bytes 921600 | tf_op jit(solution)/shard_map/all_to_all | solution.py:120
  556.6 11.8 %gather_fusion.2 = f32[2048]{0:T(1024)S(1)} fusion(f32[5760]{0:T(1024)S(1)} %mul.456, s32[2048]{0:T(1024)S(1)} %broadcast_clamp_fusion), kind=kCustom, calls=%fused_computation.2 | custom fusion | bytes 24576 | tf_op jit(solution)/shard_map/gather | solution.py:124
  568.5 24.4 %all_to_all.98 = f32[128,1,16]{2,1,0:T(1,128)S(1)} all-to-all(f32[128,1,16]{2,1,0:T(1,128)S(1)} %bitcast.129), channel_id=1, replica_groups=mesh['mem'=8,'tile'=16] {'mem','tile'}, dimensions={0} | all-to-all | bytes 16384 | tf_op jit(solution)/shard_map/all_to_all | solution.py:125
  604.7 13.9 %all_to_all.99 = f32[128,1,16]{2,1,0:T(1,128)S(1)} all-to-all(f32[128,1,16]{2,1,0:T(1,128)S(1)} %copy.114), channel_id=1, replica_groups=mesh['mem'=8,'tile'=16] {'mem','tile'}, dimensions={0} | all-to-all | bytes 16384 | tf_op jit(solution)/shard_map/all_to_all | solution.py:129
  619.4 11.4 %scatter_custom_fusion.1 = f32[5760]{0:T(1024)S(1)} fusion(s32[2048]{0:T(1024)} %bitcast.137, f32[2048]{0:T(1024)S(1)} %reshape.216, f32[]{:T(128)} %constant.17.clone.1), kind=kCustom, calls=%fused_computation.202 | custom fusion | flops 2048 | bytes 23552 | tf_op jit(solution)/shard_map/scatter-add | solution.py:133
  631.2 15.3 %all_to_all.100 = bf16[40,4,8,180]{3,2,1,0:T(8,128)(2,1)S(1)} all-to-all(bf16[40,4,8,180]{3,2,1,0:T(8,128)(2,1)S(1)} %fusion.19), channel_id=1, replica_groups=mesh['mem'=8,'tile'=16] {'mem'}, dimensions={0} | all-to-all | bytes 921600 | tf_op jit(solution)/shard_map/all_to_all | solution.py:137
  688.4 76.4 %psum.31 = f32[]{:T(128)} all-reduce(f32[]{:T(128)} %get-tuple-element.4), channel_id=1, replica_groups=mesh['mem'=8,'tile'=16] {'mem','tile'}, use_global_device_ids=true, to_apply=%region_19.20 | all-reduce | flops 1 | bytes 8 | tf_op jit(solution)/shard_map/psum | solution.py:115
  (345 shorter events, 274.3 us)
Async XLA Ops:
  7.8 54.2 %all-to-all-start.1 = ((s32[128,1,16]{2,1,0:T(1,128)}), s32[128,1,16]{2,1,0:T(1,128)S(1)}, u32[]{:S(2)}, u32[]{:S(2)}) async-start(s32[128,1,16]{2,1,0:T(1,128)} %copy.101), calls=%async_computation.1 | async-start | bytes 131072 | tf_op jit(solution)/shard_map/all_to_all | solution.py:109
  20.3 51.9 %collective-permute-start.2 = (f32[5,4,1,1440]{3,2,1,0:T(1,128)}, f32[5,4,1,1440]{3,2,1,0:T(1,128)}, u32[]{:S(2)}, u32[]{:S(2)}) collective-permute-start(f32[5,4,1,1440]{3,2,1,0:T(1,128)} %get-tuple-element.43), channel_id=1, source_target_pairs={{1,0},{2,1},{3,2},{4,3},{5,4},{6,5},{7,6},{8,7},{9,8},{10,9},{11,1... | collective-permute-start | bytes 345608 | tf_op jit(solution)/shard_map/ppermute | solution.py:24
  21.5 50.6 %collective-permute-start.3 = (f32[5,4,1,1440]{3,2,1,0:T(1,128)}, f32[5,4,1,1440]{3,2,1,0:T(1,128)}, u32[]{:S(2)}, u32[]{:S(2)}) collective-permute-start(f32[5,4,1,1440]{3,2,1,0:T(1,128)} %get-tuple-element.42), channel_id=1, source_target_pairs={{0,1},{1,2},{2,3},{3,4},{4,5},{5,6},{6,7},{7,8},{8,9},{9,10},{10,1... | collective-permute-start | bytes 345608 | tf_op jit(solution)/shard_map/ppermute | solution.py:21
  26.2 43.5 %collective-permute-start.1 = (f32[3,1,1440]{2,1,0:T(1,128)S(1)}, f32[3,1,1440]{2,1,0:T(1,128)S(1)}, u32[]{:S(2)}, u32[]{:S(2)}) collective-permute-start(f32[3,1,1440]{2,1,0:T(1,128)S(1)} %get-tuple-element.47), channel_id=1, source_target_pairs={{1,0},{2,1},{3,2},{4,3},{5,4},{6,5},{7,6},{8,7},{9,8},{10,9},{11,1... | collective-permute-start | bytes 51848 | tf_op jit(solution)/shard_map/ppermute | solution.py:24
  27.5 42.2 %collective-permute-start = (f32[3,1,1440]{2,1,0:T(1,128)S(1)}, f32[3,1,1440]{2,1,0:T(1,128)S(1)}, u32[]{:S(2)}, u32[]{:S(2)}) collective-permute-start(f32[3,1,1440]{2,1,0:T(1,128)S(1)} %get-tuple-element.46), channel_id=1, source_target_pairs={{0,1},{1,2},{2,3},{3,4},{4,5},{5,6},{6,7},{7,8},{8,9},{9,10},{10,1... | collective-permute-start | bytes 51848 | tf_op jit(solution)/shard_map/ppermute | solution.py:21
  62.0 58.9 %all-to-all-start = ((bf16[8,2,14400]{2,1,0:T(2,128)(2,1)}), bf16[8,2,14400]{2,1,0:T(2,128)(2,1)}, u32[]{:S(2)}, u32[]{:S(2)}) async-start(bf16[8,2,14400]{2,1,0:T(2,128)(2,1)} %reshape.273), calls=%async_computation | async-start | bytes 925696 | tf_op jit(solution)/shard_map/all_to_all | solution.py:112
  74.7 6.6 collective-permute-start.4
  83.7 6.4 collective-permute-start.6
  85.0 6.6 collective-permute-start.7
  93.0 7.7 %collective-permute-start.8 = (f32[5,4,1,1440]{3,2,1,0:T(1,128)S(1)}, f32[5,4,1,1440]{3,2,1,0:T(1,128)S(1)}, u32[]{:S(2)}, u32[]{:S(2)}) collective-permute-start(f32[5,4,1,1440]{3,2,1,0:T(1,128)S(1)} %get-tuple-element.37), channel_id=1, source_target_pairs={{1,0},{2,1},{3,2},{4,3},{5,4},{6,5},{7,6},{8,7},{9,8},{10,9},{11,1... | collective-permute-start | bytes 345608 | tf_op jit(solution)/shard_map/ppermute | solution.py:24
  94.3 7.8 %collective-permute-start.9 = (f32[5,4,1,1440]{3,2,1,0:T(1,128)S(1)}, f32[5,4,1,1440]{3,2,1,0:T(1,128)S(1)}, u32[]{:S(2)}, u32[]{:S(2)}) collective-permute-start(f32[5,4,1,1440]{3,2,1,0:T(1,128)S(1)} %get-tuple-element.36), channel_id=1, source_target_pairs={{0,1},{1,2},{2,3},{3,4},{4,5},{5,6},{6,7},{7,8},{8,9},{9,10},{10,1... | collective-permute-start | bytes 345608 | tf_op jit(solution)/shard_map/ppermute | solution.py:21
  120.8 28.7 %all-to-all-start.2 = ((bf16[8,2,14400]{2,1,0:T(2,128)(2,1)}), bf16[8,2,14400]{2,1,0:T(2,128)(2,1)S(1)}, u32[]{:S(2)}, u32[]{:S(2)}) async-start(bf16[8,2,14400]{2,1,0:T(2,128)(2,1)} %reshape.275), calls=%async_computation.2 | async-start | bytes 925696 | tf_op jit(solution)/shard_map/all_to_all | solution.py:120
  224.5 14.6 %all-to-all-start.4 = ((f32[128,1,16]{2,1,0:T(1,128)}), f32[128,1,16]{2,1,0:T(1,128)S(1)}, u32[]{:S(2)}, u32[]{:S(2)}) async-start(f32[128,1,16]{2,1,0:T(1,128)} %copy.107), calls=%async_computation.4 | async-start | bytes 131072 | tf_op jit(solution)/shard_map/all_to_all | solution.py:129
  254.4 15.9 %all-to-all-start.5 = ((bf16[40,4,8,180]{3,2,1,0:T(8,128)(2,1)}), bf16[40,4,8,180]{3,2,1,0:T(8,128)(2,1)}, u32[]{:S(2)}, u32[]{:S(2)}) async-start(bf16[40,4,8,180]{3,2,1,0:T(8,128)(2,1)} %fusion.17), calls=%async_computation.5 | async-start | bytes 1310720 | tf_op jit(solution)/shard_map/all_to_all | solution.py:137
  286.0 6.3 collective-permute-start.13
  293.7 6.3 collective-permute-start.14
  295.0 6.5 collective-permute-start.15
  304.4 6.3 collective-permute-start.17
  471.5 6.3 collective-permute-start.21
  479.3 6.3 collective-permute-start.22
  480.6 6.5 collective-permute-start.23
  659.8 6.3 collective-permute-start.28
  668.8 6.3 collective-permute-start.30
  670.1 6.5 collective-permute-start.31
  (54 other events, 616.5 us)
where the time goes:
time: 782 us; the launch traced here: 770 us
  blocking collectives  317 us (41%)
  local copies, waits for them, and re-layouts  204 us (26%)
  starting transfers between devices  133 us (17%)
  other arithmetic  70.1 us (9%)
  waiting for transfers between devices  39.1 us (5%)
    psum x3, blocking collectives, global_sum(): return lax.psum(value, ('mem', 'tile'))  218 us
    unnamed x88, local copies, waits for them, and re-layouts  94.7 us
    ppermute x17, starting transfers between devices, with_halo(): lax.ppermute(lax.slice_in_dim(block, block.shape[dim] - width, None, axis...  76.2 us
    all_to_all x2, blocking collectives, shards(): lax.all_to_all(picked, ('mem', 'tile'), split_axis=0, concat_axis=0, tile...  53.3 us
    gather x2, local copies, waits for them, and re-layouts, shards(): picked = increment.reshape(-1)[wanted].reshape(devices, capacity)  23.6 us
    scatter-add x2, other arithmetic, shards(): adjoint = jnp.zeros((increment.size,), jnp.float32).at[wanted].add(arrive...  22.8 us
    ppermute x17, starting transfers between devices, with_halo(): lax.ppermute(lax.slice_in_dim(block, 0, width, axis=dim), axis, backward)  21.9 us
    ppermute x17, waiting for transfers between devices, with_halo(): lax.ppermute(lax.slice_in_dim(block, block.shape[dim] - width, None, axis...  21.8 us
  transfers between devices with their start and end apart: 39, of which 18 were waited for; matrix products, arithmetic and copies ran while one was open for 12% of the time, Pallas kernels for 0%

commit v1 on v0

v1 whole, which is shorter than its diff:
```python
import functools
import math

import jax
import jax.numpy as jnp
from jax import lax
from jax.experimental import pallas as pl
from jax.experimental.pallas import tpu as pltpu
from jax.sharding import PartitionSpec as P

MESH = pl.DeviceIdType.MESH
F32 = jnp.float32
BF16 = jnp.bfloat16

FIELDS = 4
LEVELS = 2
PASSES = 4
ITERS = 2
CORRELATION = 0.6
MEMBERS_DEV = 5
MEMBERS = 40
ROWS = 8
LONS = 1440
BLOCK = 180
SLOTS = 16
SEGMENT = 1024
NM = 8
NT = 16

HALO = 4
EXT = ROWS + 2 * HALO
PLANES = MEMBERS_DEV * FIELDS
PAD = 24
GROUPS = PAD // 8
WIDE = 1536
OWN = HALO * PAD
EDGE = HALO * PAD
DEVS = NM * NT

IDS = 0


def widen(x):
    return jnp.concatenate([x, x[:, :64], x[:, 1408:1440]], axis=1)


def split(x):
    high = x.astype(BF16).astype(F32)
    return high, x - high


def fold(x, valid):
    total = x[:, 0:128]
    for k in range(1, WIDE // 128 - 1):
        total = total + x[:, 128 * k : 128 * (k + 1)]
    return total + x[:, WIDE - 128 : WIDE] * valid


def row_tile(r, g=0):
    return pl.ds(pl.multiple_of(r * PAD + g * 8, 8), 8)


def body(
    dir_ref,
    res_ref,
    sol_ref,
    ens_ref,
    east_ref,
    north_ref,
    sea_ref,
    counts_ref,
    meta_ref,
    out_sol,
    out_res,
    d_ref,
    r_ref,
    im_ref,
    x_ref,
    y_ref,
    em_ref,
    e_ref,
    n_ref,
    s_ref,
    lb_ref,
    oh_ref,
    rf_ref,
    ct_ref,
    pk_ref,
    ob_ref,
    adj_ref,
    ax_ref,
    one_q,
    one_t,
    pass_ref,
    hs_ref,
    hr_ref,
    as_ref,
    ar_ref,
    cs_ref,
    cr_ref,
    ms_ref,
    mr_ref,
    ts_ref,
    tr_ref,
    h_send,
    h_recv,
    a_send,
    a_recv,
    c_send,
    c_recv,
    m_send,
    m_recv,
    t_send,
    t_recv,
):
    m = lax.axis_index("mem")
    t = lax.axis_index("tile")
    up = lax.rem(t + 1, NT)
    down = lax.rem(t + NT - 1, NT)
    weight = 1.0 / math.sqrt(MEMBERS - 1)

    barrier = pltpu.get_barrier_semaphore()

    def greet_mem(k, _):
        pl.semaphore_signal(
            barrier, inc=1, device_id=(lax.rem(m + k, NM), t), device_id_type=MESH
        )
        return 0

    def greet_tile(k, _):
        pl.semaphore_signal(
            barrier, inc=1, device_id=(m, lax.rem(t + k, NT)), device_id_type=MESH
        )
        return 0

    lax.fori_loop(1, NM, greet_mem, 0)
    lax.fori_loop(1, NT, greet_tile, 0)

    def mem_start(i, pick):
        def one(k, _):
            peer = lax.rem(m + k, NM)
            pltpu.make_async_remote_copy(
                src_ref=ms_ref.at[i, peer if pick else 0],
                dst_ref=mr_ref.at[i, m],
                send_sem=m_send.at[i],
                recv_sem=m_recv.at[i],
                device_id=(peer, t),
                device_id_type=MESH,
            ).start()
            return 0

        lax.fori_loop(1, NM, one, 0)
        mr_ref[i, m] = ms_ref[i, m if pick else 0]

    def mem_wait(i):
        ref = mr_ref.at[i, pl.ds(0, NM - 1)]
        pltpu.make_async_copy(ref, ref, m_recv.at[i]).wait()

    def tile_start(i, pick):
        def one(k, _):
            peer = lax.rem(t + k, NT)
            pltpu.make_async_remote_copy(
                src_ref=ts_ref.at[i, peer if pick else 0],
                dst_ref=tr_ref.at[i, t],
                send_sem=t_send.at[i],
                recv_sem=t_recv.at[i],
                device_id=(m, peer),
                device_id_type=MESH,
            ).start()
            return 0

        lax.fori_loop(1, NT, one, 0)
        tr_ref[i, t] = ts_ref[i, t if pick else 0]

    def tile_wait(i):
        ref = tr_ref.at[i, pl.ds(0, NT - 1)]
        pltpu.make_async_copy(ref, ref, t_recv.at[i]).wait()

    def sides(send, recv, ssem, rsem, i):
        low = pltpu.make_async_remote_copy(
            src_ref=send.at[i, 0],
            dst_ref=recv.at[i, 1],
            send_sem=ssem.at[i, 0],
            recv_sem=rsem.at[i, 1],
            device_id=(m, down),
            device_id_type=MESH,
        )
        high = pltpu.make_async_remote_copy(
            src_ref=send.at[i, 1],
            dst_ref=recv.at[i, 0],
            send_sem=ssem.at[i, 1],
            recv_sem=rsem.at[i, 0],
            device_id=(m, up),
            device_id_type=MESH,
        )
        return low, high

    def sides_start(*which):
        for copy in sides(*which):
            copy.start()

    def sides_wait(*which):
        for copy in sides(*which):
            copy.wait_recv()

    halos = (hs_ref, hr_ref, h_send, h_recv)
    edges = (as_ref, ar_ref, a_send, a_recv)
    faces = (cs_ref, cr_ref, c_send, c_recv)
    DIR, ENS, RES, IMG = 0, 1, 2, 3

    def halo_send(src, kind):
        hs_ref[kind, 0] = src[pl.ds(OWN, EDGE), :].astype(BF16)
        hs_ref[kind, 1] = src[pl.ds(OWN + HALO * PAD, EDGE), :].astype(BF16)
        sides_start(*halos, kind)

    def halo_take(kind, dst):
        dst[pl.ds(0, EDGE), :] = hr_ref[kind, 0].astype(F32)
        dst[pl.ds(OWN + ROWS * PAD, EDGE), :] = hr_ref[kind, 1].astype(F32)

    sub = lax.broadcasted_iota(jnp.int32, (8, WIDE), 0)
    lane = lax.broadcasted_iota(jnp.int32, (8, 128), 1)
    valid = (lane < LONS - (WIDE - 128)).astype(F32)
    sub_small = lax.broadcasted_iota(jnp.int32, (8, 128), 0)
    low_half = sub < 4

    sea = widen(sea_ref[...].astype(F32))
    east = widen(east_ref[...])
    north = widen(north_ref[...])
    sea_up = pltpu.roll(sea, 7, 0)
    east_face = east * sea * pltpu.roll(sea, WIDE - 1, 1)
    north_raw = north * sea
    north_face = jnp.where(sub < 7, north_raw * sea_up, north_raw)
    cs_ref[0, 1] = jnp.where(low_half, pltpu.roll(east_face, 4, 0), north_face)
    cs_ref[0, 0] = jnp.where(
        low_half, east_face, jnp.where(sub < 7, pltpu.roll(north_face, 4, 0), sea_up)
    )

    def spread_row(value, i):
        return jnp.broadcast_to(value[i : i + 1, :], (8, WIDE))

    for i in range(ROWS):
        e_ref[pl.ds((HALO + i) * 8, 8), :] = spread_row(east_face, i)
        n_ref[pl.ds((HALO + i) * 8, 8), :] = spread_row(north_face, i)
        s_ref[pl.ds(i * 8, 8), :] = spread_row(sea, i)

    field_of = lax.rem(sub_small, 4)
    c0, c1, c2, c3 = (counts_ref[0], counts_ref[1], counts_ref[2], counts_ref[3])
    count = jnp.where(
        field_of == 0, c0, jnp.where(field_of == 1, c1, jnp.where(field_of == 2, c2, c3))
    )
    for k in range(PASSES):
        pass_ref[k] = (count > k).astype(F32)

    zero_tile = jnp.zeros((8, WIDE), F32)

    def rows_first(ref, g):
        parts = [widen(ref[8 * g + i].astype(F32)) for i in range(min(8, PLANES - 8 * g))]
        parts += [zero_tile] * (8 - len(parts))
        return jnp.stack(parts, axis=0).transpose(1, 0, 2)

    def planes_first(ref, g):
        rows = jnp.stack([ref[row_tile(HALO + i, g), :] for i in range(ROWS)], axis=0)
        return rows.transpose(1, 0, 2)[:, :, :LONS]

    def sea_rows(r):
        return s_ref[pl.ds(pl.multiple_of(r * 8, 8), 8), :]

    for g in range(GROUPS):
        turned = rows_first(dir_ref, g)
        for i in range(ROWS):
            d_ref[row_tile(HALO + i, g), :] = turned[i]
            x_ref[row_tile(HALO + i, g), :] = turned[i] * sea_rows(i)

    owner = meta_ref[0:1, :].astype(jnp.int32)
    col_id = meta_ref[1:2, :]
    rf_id = meta_ref[2:3, :]
    inv_err = 1.0 / meta_ref[3:4, :]
    owner_tile = lax.rem(owner, NT)
    owner_mem = owner // NT
    dev_iota = lax.broadcasted_iota(jnp.int32, (DEVS, SEGMENT), 0)
    owns = jnp.where(dev_iota == owner, 1.0, 0.0)
    before = jnp.where(
        lax.broadcasted_iota(jnp.int32, (SEGMENT, SEGMENT), 0)
        < lax.broadcasted_iota(jnp.int32, (SEGMENT, SEGMENT), 1),
        1.0,
        0.0,
    ).astype(BF16)
    ranks = jnp.dot(owns.astype(BF16), before, preferred_element_type=F32)
    slot = jnp.sum(ranks * owns, axis=0, keepdims=True).astype(jnp.int32)
    place = owner_mem * SLOTS + slot
    one_q[...] = jnp.where(dev_iota == place, 1.0, 0.0).astype(BF16)
    t_iota = lax.rem(lax.broadcasted_iota(jnp.int32, (2 * NT, SEGMENT), 0), NT)
    t_is_high = lax.broadcasted_iota(jnp.int32, (2 * NT, SEGMENT), 0) < NT
    one_t[...] = jnp.where(t_iota == owner_tile, 1.0, 0.0)

    def to_table(high, low):
        left = one_t[...] * jnp.where(t_is_high, high, low)
        return lax.dot_general(
            left.astype(BF16), one_q[...], (((1,), (1,)), ((), ())), preferred_element_type=F32
        )

    def tile_rows(i, table):
        for k in range(NT):
            ts_ref[i, k] = jnp.broadcast_to(table[k : k + 1, :], (8, 128))

    def tile_table(i):
        return tr_ref[i][:, 0, :]

    table = to_table(col_id, rf_id)
    tile_rows(IDS, table[NT:] * 256.0 + table[:NT])

    pl.semaphore_wait(barrier, NM + NT - 2)

    sides_start(*faces, 0)
    tile_start(IDS, True)
    halo_send(x_ref, DIR)

    for g in range(GROUPS):
        turned = rows_first(ens_ref, g)
        for i in range(ROWS):
            em_ref[row_tile(HALO + i, g), :] = turned[i] * sea_rows(i)
    halo_send(em_ref, ENS)

    tile_wait(IDS)
    ms_ref[IDS, 0] = tile_table(IDS)
    mem_start(IDS, False)

    for g in range(GROUPS):
        turned = rows_first(res_ref, g)
        for i in range(ROWS):
            r_ref[row_tile(HALO + i, g), :] = turned[i]

    mem_wait(IDS)
    ids = mr_ref[IDS].reshape(DEVS, DEVS).T
    rf_all = jnp.floor(ids * (1.0 / 256.0))
    rf_ref[...] = rf_all.astype(jnp.int32)
    ct_ref[...] = (ids - rf_all * 256.0).astype(jnp.int32)

    col_iota = lax.broadcasted_iota(jnp.int32, (256, 128), 0)

    def build(b, _):
        cols = ct_ref[pl.ds(pl.multiple_of(b * SLOTS, SLOTS), SLOTS), :]
        for s in range(SLOTS):
            oh_ref[b, :, s * 128 : (s + 1) * 128] = jnp.where(
                col_iota == cols[s : s + 1, :], 1.0, 0.0
            ).astype(BF16)
        return 0

    lax.fori_loop(0, NM, build, 0)

    sides_wait(*faces, 0)
    below, above = cr_ref[0, 0], cr_ref[0, 1]
    not_first = jnp.where(t > 0, 1.0, 0.0)
    not_last = jnp.where(t < NT - 1, 1.0, 0.0)
    for i in range(HALO):
        e_ref[pl.ds(i * 8, 8), :] = spread_row(below, i)
        e_ref[pl.ds((HALO + ROWS + i) * 8, 8), :] = spread_row(above, i)
    for i in range(HALO - 1):
        n_ref[pl.ds(i * 8, 8), :] = spread_row(below, HALO + i)
        n_ref[pl.ds((HALO + ROWS + i) * 8, 8), :] = spread_row(above, HALO + i)
    n_ref[pl.ds((HALO - 1) * 8, 8), :] = (
        spread_row(below, 2 * HALO - 1) * s_ref[pl.ds(0, 8), :] * not_first
    )
    n_ref[pl.ds((HALO + ROWS - 1) * 8, 8), :] = (
        n_ref[pl.ds((HALO + ROWS - 1) * 8, 8), :] * spread_row(above, 2 * HALO - 1) * not_last
    )

    def localize():
        for k in range(PASSES):
            src, dst = (x_ref, y_ref) if k % 2 == 0 else (y_ref, x_ref)

            def row(r, _):
                keep = pass_ref[k][:, 0:1]
                here8 = pl.ds(pl.multiple_of(r * 8, 8), 8)
                back8 = pl.ds(pl.multiple_of((r - 1) * 8, 8), 8)
                e, n, s = e_ref[here8, :], n_ref[here8, :], n_ref[back8, :]
                for g in range(GROUPS):
                    a = src[row_tile(r, g), :]
                    flux = e * (pltpu.roll(a, WIDE - 1, 1) - a)
                    moved = (
                        flux
                        - pltpu.roll(flux, 1, 1)
                        + n * (src[row_tile(r + 1, g), :] - a)
                        - s * (a - src[row_tile(r - 1, g), :])
                    )
                    dst[row_tile(r, g), :] = a + keep * moved
                return 0

            lax.fori_loop(1 + k, EXT - 1 - k, row, 0)

    row_key = lax.broadcasted_iota(jnp.int32, (64, 128), 0)
    key = (row_key // 8) * FIELDS + lax.rem(row_key, 4)
    is_high = lax.rem(row_key, 8) < 4

    def window(b):
        start = BLOCK * b
        first = (start // 128) * 128
        return first, start - first

    dots = []
    norms = None
    for iteration in range(ITERS):
        base = 1 + 3 * iteration
        PICK, WGT, SUM = base, base + 1, base + 2
        if iteration == 0:
            sides_wait(*halos, DIR)
            halo_take(DIR, x_ref)
        localize()

        def partial(r, _):
            total = zero_tile
            for g in range(GROUPS):
                at = row_tile(r + HALO, g)
                total = total + em_ref[at, :] * x_ref[at, :].astype(BF16).astype(F32)
            total = total + pltpu.roll(total, 4, 0)
            high, low = split(total)
            adj_ref[pl.ds(pl.multiple_of(r * 8, 8), 8), :] = jnp.where(low_half, high, low)
            return 0

        lax.fori_loop(0, ROWS, partial, 0)
        for b in range(NM):
            first, shift = window(b)
            piece = adj_ref[:, first : first + 384]
            if shift:
                piece = pltpu.roll(piece, 384 - shift, 1)
            lb_ref[b] = piece[:, :256].astype(BF16)

        def gather(b, _):
            got = jnp.dot(lb_ref[b], oh_ref[b], preferred_element_type=F32)
            rows16 = pl.ds(pl.multiple_of(b * SLOTS, SLOTS), SLOTS)
            wanted = rf_ref[rows16, :]
            rows = []
            for s in range(SLOTS):
                part = jnp.where(
                    key == wanted[s : s + 1, :], got[:, s * 128 : (s + 1) * 128], 0.0
                )
                rows.append(jnp.sum(part, axis=0, keepdims=True))
            pk_ref[rows16, :] = jnp.concatenate(rows, axis=0)
            return 0

        lax.fori_loop(0, NM, gather, 0)
        ms_ref[PICK] = pk_ref[...].T.reshape(NM, NT, 128)
        mem_start(PICK, True)
        mem_wait(PICK)
        summed = mr_ref[PICK, 0]
        for k in range(1, NM):
            summed = summed + mr_ref[PICK, k]
        tile_rows(PICK, summed * weight)
        tile_start(PICK, True)
        if iteration == 0:
            def mask_residual(r, _):
                sea_row = s_ref[pl.ds(pl.multiple_of(r * 8, 8), 8), :]
                for g in range(GROUPS):
                    at = row_tile(r + HALO, g)
                    y_ref[at, :] = r_ref[at, :] * sea_row
                return 0

            lax.fori_loop(0, ROWS, mask_residual, 0)
        tile_wait(PICK)

        high, low = split(tile_table(PICK))
        both = jnp.concatenate([high, low], axis=0).astype(BF16)
        seen = jnp.dot(both, one_q[...], preferred_element_type=F32)
        value = jnp.sum(seen * one_t[...], axis=0, keepdims=True)
        u = value * inv_err
        along = lax.broadcasted_iota(jnp.int32, (1, SEGMENT), 1)
        following = jnp.where(along == SEGMENT - 1, 0.0, pltpu.roll(u, SEGMENT - 1, 1))
        preceding = jnp.where(along == 0, 0.0, pltpu.roll(u, 1, 1))
        ends = ((along == 0) | (along == SEGMENT - 1)).astype(F32)
        square = CORRELATION * CORRELATION
        mixed = ((1.0 + square - square * ends) * u - CORRELATION * (following + preceding)) / (
            1.0 - square
        )
        weighted = mixed * inv_err
        high, low = split(weighted)
        table = to_table(high, low)
        tile_rows(WGT, table[:NT] + table[NT:])
        tile_start(WGT, True)
        if iteration == 0:
            halo_send(y_ref, RES)
        tile_wait(WGT)
        ms_ref[WGT, 0] = tile_table(WGT)
        mem_start(WGT, False)
        mem_wait(WGT)
        pk_ref[...] = mr_ref[WGT].reshape(DEVS, DEVS).T

        def scatter(b, _):
            rows16 = pl.ds(pl.multiple_of(b * SLOTS, SLOTS), SLOTS)
            wanted = rf_ref[rows16, :]
            high, low = split(pk_ref[rows16, :])
            parts = []
            for s in range(SLOTS):
                row = jnp.where(is_high, high[s : s + 1, :], low[s : s + 1, :])
                parts.append(jnp.where(key == wanted[s : s + 1, :], row, 0.0).astype(BF16))
            ob_ref[b] = lax.dot_general(
                jnp.concatenate(parts, axis=1),
                oh_ref[b],
                (((1,), (1,)), ((), ())),
                preferred_element_type=F32,
            )
            return 0

        lax.fori_loop(0, NM, scatter, 0)
        adj_ref[...] = jnp.zeros((64, WIDE), F32)
        for b in range(NM):
            first, shift = window(b)
            piece = jnp.concatenate([ob_ref[b], jnp.zeros((64, 128), F32)], axis=1)
            if shift:
                piece = pltpu.roll(piece, shift, 1)
            adj_ref[:, first : first + 384] = adj_ref[:, first : first + 384] + piece
        lane64 = lax.broadcasted_iota(jnp.int32, (64, 128), 1)
        head, tail = adj_ref[:, 0:128], adj_ref[:, WIDE - 128 : WIDE]
        adj_ref[:, WIDE - 128 : WIDE] = jnp.where(
            lane64 < 32, tail, jnp.where(lane64 < 96, pltpu.roll(head, 32, 1), pltpu.roll(tail, 96, 1))
        )
        own_rows = []
        for i in range(ROWS):
            tile = adj_ref[pl.ds(i * 8, 8), :]
            tile = (tile + pltpu.roll(tile, 4, 0)) * weight
            ax_ref[pl.ds((HALO + i) * 8, 8), :] = tile
        for side in range(2):
            for i in range(HALO // 2):
                first = HALO + HALO * side + 2 * i
                as_ref[iteration, side, pl.ds(i * 8, 8), :] = jnp.where(
                    low_half,
                    ax_ref[pl.ds(first * 8, 8), :],
                    ax_ref[pl.ds((first + 1) * 8, 8), :],
                )
        sides_start(*edges, iteration)
        if iteration == 0:
            sides_wait(*halos, ENS)
            halo_take(ENS, em_ref)
        sides_wait(*edges, iteration)
        for side in range(2):
            for i in range(HALO // 2):
                first = (HALO + ROWS) * side + 2 * i
                packed = ar_ref[iteration, side, pl.ds(i * 8, 8), :]
                turned = pltpu.roll(packed, 4, 0)
                ax_ref[pl.ds(first * 8, 8), :] = jnp.where(low_half, packed, turned)
                ax_ref[pl.ds((first + 1) * 8, 8), :] = jnp.where(low_half, turned, packed)

        def back(r, _):
            row = ax_ref[pl.ds(pl.multiple_of(r * 8, 8), 8), :]
            for g in range(GROUPS):
                at = row_tile(r, g)
                x_ref[at, :] = (em_ref[at, :] * row).astype(BF16).astype(F32)
            return 0

        lax.fori_loop(0, EXT, back, 0)
        localize()

        def image(r, carry):
            sea_row = s_ref[pl.ds(pl.multiple_of(r * 8, 8), 8), :]
            sums = list(carry)
            for g in range(GROUPS):
                at = row_tile(r + HALO, g)
                d, res = d_ref[at, :], r_ref[at, :]
                moved = sea_row * x_ref[at, :]
                img = d + moved
                im_ref[at, :] = img
                if iteration == 0:
                    y_ref[at, :] = img * sea_row
                terms = [d * img, res * res]
                if iteration == 0:
                    terms += [res * img, img * img]
                sums = [total + fold(term, valid) for total, term in zip(sums, terms)]
            return tuple(sums)

        count_sums = 4 if iteration == 0 else 2
        sums = lax.fori_loop(0, ROWS, image, (jnp.zeros((8, 128), F32),) * count_sums)
        packed = jnp.zeros((8, 128), F32)
        for i, total in enumerate(sums):
            packed = jnp.where(sub_small == i, jnp.sum(total, axis=0, keepdims=True), packed)
        ms_ref[SUM, 0, pl.ds(0, 8), :] = packed
        ms_ref[SUM, 0, pl.ds(8, 8), :] = packed
        mem_start(SUM, False)
        if iteration == 0:
            halo_send(y_ref, IMG)
        mem_wait(SUM)
        part = mr_ref[SUM, 0, pl.ds(0, 8), :]
        for k in range(1, NM):
            part = part + mr_ref[SUM, k, pl.ds(0, 8), :]
        ts_ref[SUM, 0] = part
        tile_start(SUM, False)
        tile_wait(SUM)
        total = tr_ref[SUM, 0]
        for k in range(1, NT):
            total = total + tr_ref[SUM, k]
        total = jnp.sum(total, axis=1, keepdims=True)
        d_image, rr = total[0:1, :], total[1:2, :]
        step = rr / d_image
        if iteration == 0:
            r_image, image_image = total[2:3, :], total[3:4, :]
            fresh = rr - 2.0 * step * r_image + step * step * image_image
            beta = fresh / rr
            first_step = step
            for p in range(PLANES):
                out_sol[p] = sol_ref[p] + step * dir_ref[p]
            sides_wait(*halos, RES)
            sides_wait(*halos, IMG)
            for side in range(2):
                for i in range(HALO):
                    inner = pl.ds(i * PAD, PAD)
                    outer = pl.ds(side * (OWN + ROWS * PAD) + i * PAD, PAD)
                    mixed = (
                        hr_ref[RES, side, inner, :].astype(F32)
                        - step * hr_ref[IMG, side, inner, :].astype(F32)
                        + beta * hr_ref[DIR, side, inner, :].astype(F32)
                    )
                    x_ref[outer, :] = mixed

            def turn(r, _):
                sea_row = s_ref[pl.ds(pl.multiple_of(r * 8, 8), 8), :]
                for g in range(GROUPS):
                    at = row_tile(r + HALO, g)
                    res = r_ref[at, :] - step * im_ref[at, :]
                    r_ref[at, :] = res
                    fresh_dir = res + beta * d_ref[at, :]
                    d_ref[at, :] = fresh_dir
                    x_ref[at, :] = fresh_dir * sea_row
                return 0

            lax.fori_loop(0, ROWS, turn, 0)
        else:

            for g in range(GROUPS):
                d = planes_first(d_ref, g)
                res = planes_first(r_ref, g)
                img = planes_first(im_ref, g)
                for i in range(min(8, PLANES - 8 * g)):
                    p = 8 * g + i
                    out_sol[p] = out_sol[p] + step * d[i]
                    out_res[p] = res[i] - step * img[i]

    for i in range(1 + 3 * ITERS):
        ref = mr_ref.at[i, pl.ds(0, NM - 1)]
        pltpu.make_async_copy(ref, ref, m_send.at[i]).wait()
        ref = tr_ref.at[i, pl.ds(0, NT - 1)]
        pltpu.make_async_copy(ref, ref, t_send.at[i]).wait()
    for group, many in ((halos, 4), (edges, ITERS), (faces, 1)):
        for i in range(many):
            for copy in sides(*group, i):
                copy.wait_send()


def shards(
    solution,
    residual,
    direction,
    ensemble,
    east_rate,
    north_rate,
    sea_mask,
    pass_counts,
    obs_owner,
    obs_cell,
    obs_level,
    obs_variable,
    obs_error,
):
    def planes(x):
        return x.reshape(PLANES, ROWS, LONS)

    row, col = obs_cell // BLOCK, obs_cell % BLOCK
    key = row * FIELDS + obs_variable * LEVELS + obs_level
    meta = jnp.stack(
        [obs_owner[:, 0].astype(F32), col.astype(F32), key.astype(F32), obs_error], axis=0
    )
    exchanges = 1 + 3 * ITERS
    vmem = pl.BlockSpec(memory_space=pltpu.VMEM)
    field = pltpu.VMEM((EXT * PAD, WIDE), F32)
    band = pltpu.VMEM((EXT * 8, WIDE), F32)
    shape = jax.ShapeDtypeStruct((PLANES, ROWS, LONS), F32)
    sol, res = pl.pallas_call(
        body,
        out_shape=(shape, shape),
        in_specs=[vmem] * 7 + [pl.BlockSpec(memory_space=pltpu.SMEM), vmem],
        out_specs=(vmem, vmem),
        scratch_shapes=[
            field,
            field,
            field,
            field,
            field,
            field,
            band,
            band,
            pltpu.VMEM((ROWS * 8, WIDE), F32),
            pltpu.VMEM((NM, 64, 256), BF16),
            pltpu.VMEM((NM, 256, SLOTS * 128), BF16),
            pltpu.VMEM((DEVS, 128), jnp.int32),
            pltpu.VMEM((DEVS, 128), jnp.int32),
            pltpu.VMEM((DEVS, 128), F32),
            pltpu.VMEM((NM, 64, 256), F32),
            pltpu.VMEM((64, WIDE), F32),
            band,
            pltpu.VMEM((DEVS, SEGMENT), BF16),
            pltpu.VMEM((2 * NT, SEGMENT), F32),
            pltpu.VMEM((PASSES, 8, 128), F32),
            pltpu.VMEM((4, 2, EDGE, WIDE), BF16),
            pltpu.VMEM((4, 2, EDGE, WIDE), BF16),
            pltpu.VMEM((ITERS, 2, 16, WIDE), F32),
            pltpu.VMEM((ITERS, 2, 16, WIDE), F32),
            pltpu.VMEM((1, 2, 8, WIDE), F32),
            pltpu.VMEM((1, 2, 8, WIDE), F32),
            pltpu.VMEM((exchanges, NM, NT, 128), F32),
            pltpu.VMEM((exchanges, NM, NT, 128), F32),
            pltpu.VMEM((exchanges, NT, 8, 128), F32),
            pltpu.VMEM((exchanges, NT, 8, 128), F32),
            pltpu.SemaphoreType.DMA((4, 2)),
            pltpu.SemaphoreType.DMA((4, 2)),
            pltpu.SemaphoreType.DMA((ITERS, 2)),
            pltpu.SemaphoreType.DMA((ITERS, 2)),
            pltpu.SemaphoreType.DMA((1, 2)),
            pltpu.SemaphoreType.DMA((1, 2)),
            pltpu.SemaphoreType.DMA((exchanges,)),
            pltpu.SemaphoreType.DMA((exchanges,)),
            pltpu.SemaphoreType.DMA((exchanges,)),
            pltpu.SemaphoreType.DMA((exchanges,)),
        ],
        compiler_params=pltpu.CompilerParams(
            collective_id=0, has_side_effects=True, vmem_limit_bytes=60 * 1024 * 1024
        ),
    )(
        planes(direction),
        planes(residual),
        planes(solution),
        planes(ensemble),
        east_rate,
        north_rate,
        sea_mask,
        pass_counts,
        meta,
    )
    return sol.reshape(solution.shape), res.reshape(solution.shape)


def solution(mesh):
    return jax.shard_map(
        shards,
        mesh=mesh,
        in_specs=(
            P("mem", None, "tile", None),
            P("mem", None, "tile", None),
            P("mem", None, "tile", None),
            P("mem", None, "tile", None),
            P("tile", None),
            P("tile", None),
            P("tile", None),
            P(),
            P(("mem", "tile"), None),
            P(("mem", "tile")),
            P(("mem", "tile")),
            P(("mem", "tile")),
            P(("mem", "tile")),
        ),
        out_specs=(P("mem", None, "tile", None), P("mem", None, "tile", None)),
        check_vma=False,
    )
```

time: 782 us -> 147 us (0.19); the launches traced: 770 us -> 147 us
  blocking collectives: 317 us -> 0 us
  local copies, waits for them, and re-layouts: 204 us -> 5.31 us
  Pallas kernels: 0 us -> 140 us
  starting transfers between devices: 133 us -> 0 us
  other arithmetic: 70.1 us -> 0.65 us
  waiting for transfers between devices: 39.1 us -> 0 us
    psum x3 -> x0, blocking collectives: 218 us -> none  [global_sum(): return lax.psum(value, ('mem', 'tile'))]
    pallas_call x0 -> x1, Pallas kernels: none -> 140 us  [shards(): pl.pallas_call(body, out_shape=(shape, shape), in_specs=[vmem] * 7 + [pl....]
    all_to_all x5 -> x0, blocking collectives: 99.4 us -> none  [the longest x2 53.3 us: shards(): lax.all_to_all(picked, ('mem', 'tile'), split_axis=0, concat_axis=0, tile...]
    ppermute x34 -> x0, starting transfers between devices: 98.1 us -> none  [the longest x17 76.2 us: with_halo(): lax.ppermute(lax.slice_in_dim(block, block.shape[dim] - width, None, axis...]
    unnamed x88 -> x14, local copies, waits for them, and re-layouts: 94.7 us -> 5.31 us
    gather x4 -> x0, local copies, waits for them, and re-layouts: 37.7 us -> none  [the longest x2 23.6 us: shards(): picked = increment.reshape(-1)[wanted].reshape(devices, capacity)]
    all_to_all x5 -> x0, starting transfers between devices: 34.6 us -> none  [the longest x1 11.5 us: shards(): lax.all_to_all(send_ids, ('mem', 'tile'), split_axis=0, concat_axis=0, ti...]
    all_to_all x10 -> x0, local copies, waits for them, and re-layouts: 30.7 us -> none  [the longest x2 17.2 us: shards(): lax.all_to_all(shaped, 'mem', split_axis=3, concat_axis=0, tiled=True)]
  transfers between devices with their start and end apart: 39 -> 0, of which waited for: 18 -> 0; matrix products, arithmetic and copies ran while one was open for 12% -> 0% of each run, Pallas kernels for 0% -> 0%
where the time goes in v1:
time: 147 us
  Pallas kernels  140 us (95%)
  local copies, waits for them, and re-layouts  5.31 us (4%)
    pallas_call x1, Pallas kernels, shards(): pl.pallas_call(body, out_shape=(shape, shape), in_specs=[vmem] * 7 + [pl....  140 us
    unnamed x14, local copies, waits for them, and re-layouts  5.31 us

profile of v1, /device:TPU:1, one launch (start us, length us, event | category | flops | bytes accessed | tf_op | source)
XLA Modules:
  0.0 146.9 jit_solution(7933549292919372478)
XLA Ops:
  0.6 0.0 copy-start.4
  0.6 0.0 copy-start.3
  0.7 0.7 copy-done.4
  1.3 0.0 copy-start.1
  1.3 0.0 copy-start.2
  1.3 0.0 copy-done.3
  1.3 0.7 copy-done.1
  2.0 0.0 copy-done.2
  2.0 0.0 copy-start.5
  2.1 0.7 copy-done.5
  2.7 0.6 pad_maximum_fusion.meta_ref
  3.4 140.2 %shard_map.140 = (f32[20,8,1440]{2,1,0:T(8,128)}, f32[20,8,1440]{2,1,0:T(8,128)}) custom-call(f32[20,8,1440]{2,1,0:T(8,128)} %bitcast.13, f32[20,8,1440]{2,1,0:T(8,128)} %bitcast.14, f32[20,8,1440]{2,1,0:T(8,128)} %bitcast.15, bf16[20,8,1440]{2,1,0:T(8,128)(2,1)} %bitcast.16, f32[8,1440]{1,0:T(8,128)} %east_ref.1, f32[8,1440]{1,0:T(8,128)} %north_ref.1, ...), custom_call_target="tpu_custom_call" | custom-call | tf_op jit(solution)/shard_map/pallas_call | solution.py:674
  143.6 0.0 copy-start
  143.6 2.3 %copy.17 = f32[5,4,8,1440]{3,2,1,0:T(8,128)} copy(f32[5,4,8,1440]{3,2,1,0:T(8,128)} %bitcast.12) | data formatting | bytes 1843200
  145.9 0.0 copy-done
  145.9 0.9 copy.18
  (2 shorter events, 0.0 us)
Async XLA Ops:
  0.6 0.7 copy-start.4
  0.6 0.7 copy-start.3
  1.3 0.7 copy-start.1
  1.3 0.7 copy-start.2
  2.0 0.7 copy-start.5
  143.6 2.3 %copy-start = (f32[20,8,1440]{2,1,0:T(8,128)S(1)}, f32[20,8,1440]{2,1,0:T(8,128)}, u32[]{:S(2)}) copy-start(f32[20,8,1440]{2,1,0:T(8,128)} %get-tuple-element.5) | copy-start | bytes 2764804

commit v2 on v1

--- a/solution.py
+++ b/solution.py
@@ -36,6 +36,8 @@
 OWN = HALO * PAD
 EDGE = HALO * PAD
 DEVS = NM * NT
+LIMIT = 60 * 1024 * 1024
+TILES = WIDE // 128
 
 IDS = 0
 
@@ -56,11 +58,30 @@
     return total + x[:, WIDE - 128 : WIDE] * valid
 
 
+def cols_of(j):
+    return slice(128 * j, 128 * (j + 1))
+
+
 def row_tile(r, g=0):
     return pl.ds(pl.multiple_of(r * PAD + g * 8, 8), 8)
 
 
 def body(
+    dir_hbm,
+    res_hbm,
+    sol_hbm,
+    ens_hbm,
+    east_hbm,
+    north_hbm,
+    sea_hbm,
+    counts_ref,
+    owner_hbm,
+    cell_hbm,
+    level_hbm,
+    variable_hbm,
+    error_hbm,
+    out_sol,
+    out_res,
     dir_ref,
     res_ref,
     sol_ref,
@@ -68,18 +89,27 @@
     east_ref,
     north_ref,
     sea_ref,
-    counts_ref,
-    meta_ref,
-    out_sol,
-    out_res,
+    owner_ref,
+    cell_ref,
+    level_ref,
+    variable_ref,
+    error_ref,
+    load_sem,
     d_ref,
     r_ref,
     im_ref,
     x_ref,
-    y_ref,
+    p1_ref,
+    p2_ref,
+    p3_ref,
+    z_ref,
+    l0_ref,
+    lr_ref,
     em_ref,
     e_ref,
     n_ref,
+    w_ref,
+    k_ref,
     s_ref,
     lb_ref,
     oh_ref,
@@ -119,6 +149,30 @@
     down = lax.rem(t + NT - 1, NT)
     weight = 1.0 / math.sqrt(MEMBERS - 1)
 
+    loads = {}
+    for i, (name, source, target) in enumerate(
+        (
+            ("dir", dir_hbm, dir_ref),
+            ("sea", sea_hbm, sea_ref),
+            ("east", east_hbm, east_ref),
+            ("north", north_hbm, north_ref),
+            ("owner", owner_hbm, owner_ref),
+            ("cell", cell_hbm, cell_ref),
+            ("level", level_hbm, level_ref),
+            ("variable", variable_hbm, variable_ref),
+            ("error", error_hbm, error_ref),
+            ("ens", ens_hbm, ens_ref),
+            ("res", res_hbm, res_ref),
+            ("sol", sol_hbm, sol_ref),
+        )
+    ):
+        loads[name] = pltpu.make_async_copy(source, target, load_sem.at[i])
+        loads[name].start()
+
+    def loaded(*which):
+        for name in which:
+            loads[name].wait()
+
     barrier = pltpu.get_barrier_semaphore()
 
     def greet_mem(k, _):
@@ -203,26 +257,58 @@
         for copy in sides(*which):
             copy.wait_recv()
 
-    halos = (hs_ref, hr_ref, h_send, h_recv)
     edges = (as_ref, ar_ref, a_send, a_recv)
     faces = (cs_ref, cr_ref, c_send, c_recv)
     DIR, ENS, RES, IMG = 0, 1, 2, 3
 
-    def halo_send(src, kind):
-        hs_ref[kind, 0] = src[pl.ds(OWN, EDGE), :].astype(BF16)
-        hs_ref[kind, 1] = src[pl.ds(OWN + HALO * PAD, EDGE), :].astype(BF16)
-        sides_start(*halos, kind)
-
-    def halo_take(kind, dst):
-        dst[pl.ds(0, EDGE), :] = hr_ref[kind, 0].astype(F32)
-        dst[pl.ds(OWN + ROWS * PAD, EDGE), :] = hr_ref[kind, 1].astype(F32)
+    def halo_piece(kind, dist):
+        low = pltpu.make_async_remote_copy(
+            src_ref=hs_ref.at[kind, 0, dist - 1],
+            dst_ref=hr_ref.at[kind, 1, dist - 1],
+            send_sem=h_send.at[kind, dist - 1, 0],
+            recv_sem=h_recv.at[kind, dist - 1, 1],
+            device_id=(m, down),
+            device_id_type=MESH,
+        )
+        high = pltpu.make_async_remote_copy(
+            src_ref=hs_ref.at[kind, 1, dist - 1],
+            dst_ref=hr_ref.at[kind, 0, dist - 1],
+            send_sem=h_send.at[kind, dist - 1, 1],
+            recv_sem=h_recv.at[kind, dist - 1, 0],
+            device_id=(m, up),
+            device_id_type=MESH,
+        )
+        return low, high
+
+    def below_row(dist):
+        return HALO - dist
+
+    def above_row(dist):
+        return HALO + ROWS - 1 + dist
+
+    def whole_row(r):
+        return pl.ds(r * PAD, PAD)
+
+    def halo_send(kind, dist, row_of):
+        hs_ref[kind, 0, dist - 1] = row_of(HALO + dist - 1).astype(BF16)
+        hs_ref[kind, 1, dist - 1] = row_of(HALO + ROWS - dist).astype(BF16)
+        for copy in halo_piece(kind, dist):
+            copy.start()
+
+    def halo_take(kind, dist, dst):
+        for copy in halo_piece(kind, dist):
+            copy.wait_recv()
+        dst[whole_row(below_row(dist)), :] = hr_ref[kind, 0, dist - 1].astype(F32)
+        dst[whole_row(above_row(dist)), :] = hr_ref[kind, 1, dist - 1].astype(F32)
 
     sub = lax.broadcasted_iota(jnp.int32, (8, WIDE), 0)
     lane = lax.broadcasted_iota(jnp.int32, (8, 128), 1)
     valid = (lane < LONS - (WIDE - 128)).astype(F32)
     sub_small = lax.broadcasted_iota(jnp.int32, (8, 128), 0)
     low_half = sub < 4
-
+    is_first, is_last = lane == 0, lane == 127
+
+    loaded("sea", "east", "north")
     sea = widen(sea_ref[...].astype(F32))
     east = widen(east_ref[...])
     north = widen(north_ref[...])
@@ -265,16 +351,30 @@
     def sea_rows(r):
         return s_ref[pl.ds(pl.multiple_of(r * 8, 8), 8), :]
 
+    loaded("dir")
     for g in range(GROUPS):
         turned = rows_first(dir_ref, g)
         for i in range(ROWS):
             d_ref[row_tile(HALO + i, g), :] = turned[i]
             x_ref[row_tile(HALO + i, g), :] = turned[i] * sea_rows(i)
 
-    owner = meta_ref[0:1, :].astype(jnp.int32)
-    col_id = meta_ref[1:2, :]
-    rf_id = meta_ref[2:3, :]
-    inv_err = 1.0 / meta_ref[3:4, :]
+    pl.semaphore_wait(barrier, NM + NT - 2)
+
+    sides_start(*faces, 0)
+
+    def masked(ref):
+        return lambda r: ref[whole_row(r), :]
+
+    halo_send(DIR, 1, masked(x_ref))
+    halo_send(DIR, 2, masked(x_ref))
+
+    loaded("owner", "cell", "level", "variable", "error")
+    owner = owner_ref[...]
+    cell = cell_ref[...].astype(F32)
+    cell_row = jnp.floor((cell + 0.5) * (1.0 / BLOCK))
+    col_id = cell - cell_row * BLOCK
+    rf_id = cell_row * FIELDS + (variable_ref[...] * LEVELS + level_ref[...]).astype(F32)
+    inv_err = 1.0 / error_ref[...]
     owner_tile = lax.rem(owner, NT)
     owner_mem = owner // NT
     dev_iota = lax.broadcasted_iota(jnp.int32, (DEVS, SEGMENT), 0)
@@ -309,44 +409,26 @@
     table = to_table(col_id, rf_id)
     tile_rows(IDS, table[NT:] * 256.0 + table[:NT])
 
-    pl.semaphore_wait(barrier, NM + NT - 2)
-
-    sides_start(*faces, 0)
     tile_start(IDS, True)
-    halo_send(x_ref, DIR)
-
+    halo_send(DIR, 3, masked(x_ref))
+    halo_send(DIR, 4, masked(x_ref))
+
+    loaded("res")
+    for g in range(GROUPS):
+        turned = rows_first(res_ref, g)
+        for i in range(ROWS):
+            r_ref[row_tile(HALO + i, g), :] = turned[i]
+            lr_ref[row_tile(HALO + i, g), :] = turned[i] * sea_rows(i)
+    for dist in range(1, HALO + 1):
+        halo_send(RES, dist, masked(lr_ref))
+
+    loaded("ens")
     for g in range(GROUPS):
         turned = rows_first(ens_ref, g)
         for i in range(ROWS):
             em_ref[row_tile(HALO + i, g), :] = turned[i] * sea_rows(i)
-    halo_send(em_ref, ENS)
-
-    tile_wait(IDS)
-    ms_ref[IDS, 0] = tile_table(IDS)
-    mem_start(IDS, False)
-
-    for g in range(GROUPS):
-        turned = rows_first(res_ref, g)
-        for i in range(ROWS):
-            r_ref[row_tile(HALO + i, g), :] = turned[i]
-
-    mem_wait(IDS)
-    ids = mr_ref[IDS].reshape(DEVS, DEVS).T
-    rf_all = jnp.floor(ids * (1.0 / 256.0))
-    rf_ref[...] = rf_all.astype(jnp.int32)
-    ct_ref[...] = (ids - rf_all * 256.0).astype(jnp.int32)
-
-    col_iota = lax.broadcasted_iota(jnp.int32, (256, 128), 0)
-
-    def build(b, _):
-        cols = ct_ref[pl.ds(pl.multiple_of(b * SLOTS, SLOTS), SLOTS), :]
-        for s in range(SLOTS):
-            oh_ref[b, :, s * 128 : (s + 1) * 128] = jnp.where(
-                col_iota == cols[s : s + 1, :], 1.0, 0.0
-            ).astype(BF16)
-        return 0
-
-    lax.fori_loop(0, NM, build, 0)
+    for dist in range(1, HALO + 1):
+        halo_send(ENS, dist, masked(em_ref))
 
     sides_wait(*faces, 0)
     below, above = cr_ref[0, 0], cr_ref[0, 1]
@@ -365,28 +447,102 @@
         n_ref[pl.ds((HALO + ROWS - 1) * 8, 8), :] * spread_row(above, 2 * HALO - 1) * not_last
     )
 
-    def localize():
+    for r in range(1, EXT - 1):
+        here = pl.ds(r * 8, 8)
+        e, n, s = e_ref[here, :], n_ref[here, :], n_ref[pl.ds((r - 1) * 8, 8), :]
+        w = pltpu.roll(e, 1, 1)
+        w_ref[here, :] = w
+        k_ref[here, :] = 1.0 - e - w - n - s
+
+    levels = (x_ref, p1_ref, p2_ref, p3_ref)
+
+    def localization(result):
+        def passing(k, first, second):
+            src = levels[k]
+            dst = levels[k + 1] if k + 1 < PASSES else result
+            keep = jnp.broadcast_to(pass_ref[k][:, 0:1], (8, 128)) > 0.0
+
+            def row(r):
+                here8 = pl.multiple_of(r * 8, 8)
+                back8 = pl.multiple_of((r - 1) * 8, 8)
+                ats = [(row_tile(r, g), row_tile(r + 1, g), row_tile(r - 1, g)) for g in range(GROUPS)]
+                near, far, last = [], [], []
+                for at, _, _ in ats:
+                    v = src[at, cols_of(0)]
+                    near.append((v, pltpu.roll(v, 1, 1), pltpu.roll(v, 127, 1)))
+                    last.append(pltpu.roll(src[at, cols_of(TILES - 1)], 1, 1))
+                first_east = [x[2] for x in near]
+                for j in range(TILES):
+                    cols = cols_of(j)
+                    here, back = pl.ds(here8, 8), pl.ds(back8, 8)
+                    ck, ce, cw = k_ref[here, cols], e_ref[here, cols], w_ref[here, cols]
+                    cn, cs = n_ref[here, cols], n_ref[back, cols]
+                    for g, (at, over, under) in enumerate(ats):
+                        v, west, east = near[g]
+                        if j < TILES - 1:
+                            ahead = src[at, cols_of(j + 1)]
+                            following = (ahead, pltpu.roll(ahead, 1, 1), pltpu.roll(ahead, 127, 1))
+                            next_east = following[2]
+                        else:
+                            following, next_east = None, first_east[g]
+                        total = (
+                            ck * v
+                            + ce * jnp.where(is_last, next_east, east)
+                            + cw * jnp.where(is_first, last[g], west)
+                            + cn * src[over, cols]
+                            + cs * src[under, cols]
+                        )
+                        dst[at, cols] = jnp.where(keep, total, v)
+                        near[g], last[g] = following, west
+
+            row(first)
+            row(second)
+
+        def across(k, low, high):
+            def pair(i, _):
+                passing(k, low + 2 * i, low + 2 * i + 1)
+                return 0
+
+            lax.fori_loop(0, (high - low) // 2, pair, 0)
+
+        return passing, across
+
+    def localize_pass(result, k):
+        localization(result)[1](k, 1 + k, EXT - 1 - k)
+
+    def localize(result):
         for k in range(PASSES):
-            src, dst = (x_ref, y_ref) if k % 2 == 0 else (y_ref, x_ref)
-
-            def row(r, _):
-                keep = pass_ref[k][:, 0:1]
-                here8 = pl.ds(pl.multiple_of(r * 8, 8), 8)
-                back8 = pl.ds(pl.multiple_of((r - 1) * 8, 8), 8)
-                e, n, s = e_ref[here8, :], n_ref[here8, :], n_ref[back8, :]
-                for g in range(GROUPS):
-                    a = src[row_tile(r, g), :]
-                    flux = e * (pltpu.roll(a, WIDE - 1, 1) - a)
-                    moved = (
-                        flux
-                        - pltpu.roll(flux, 1, 1)
-                        + n * (src[row_tile(r + 1, g), :] - a)
-                        - s * (a - src[row_tile(r - 1, g), :])
-                    )
-                    dst[row_tile(r, g), :] = a + keep * moved
-                return 0
-
-            lax.fori_loop(1 + k, EXT - 1 - k, row, 0)
+            localize_pass(result, k)
+
+    def localize_stage(result, stage):
+        passing, across = localization(result)
+        for k in range(stage):
+            dist = stage - 1 - k
+            if dist:
+                passing(k, below_row(dist), above_row(dist))
+            else:
+                across(k, HALO, HALO + ROWS)
+
+
+    col_iota = lax.broadcasted_iota(jnp.int32, (256, 128), 0).astype(F32).astype(BF16)
+    ones, zeros = jnp.ones((256, 128), BF16), jnp.zeros((256, 128), BF16)
+
+    def build_one_hots():
+        mem_wait(IDS)
+        ids = mr_ref[IDS].reshape(DEVS, DEVS).T
+        rf_all = jnp.floor(ids * (1.0 / 256.0))
+        rf_ref[...] = rf_all.astype(jnp.int32)
+        ct_ref[...] = ids - rf_all * 256.0
+
+        def build(b, _):
+            cols = ct_ref[pl.ds(pl.multiple_of(b * SLOTS, SLOTS), SLOTS), :]
+            for s in range(SLOTS):
+                same = jnp.broadcast_to(cols[s : s + 1, :], (16, 128)).astype(BF16)
+                same = jnp.concatenate([same] * 16, axis=0)
+                oh_ref[b, :, s * 128 : (s + 1) * 128] = jnp.where(col_iota == same, ones, zeros)
+            return 0
+
+        lax.fori_loop(0, NM, build, 0)
 
     row_key = lax.broadcasted_iota(jnp.int32, (64, 128), 0)
     key = (row_key // 8) * FIELDS + lax.rem(row_key, 4)
@@ -397,21 +553,27 @@
         first = (start // 128) * 128
         return first, start - first
 
-    dots = []
-    norms = None
     for iteration in range(ITERS):
         base = 1 + 3 * iteration
         PICK, WGT, SUM = base, base + 1, base + 2
         if iteration == 0:
-            sides_wait(*halos, DIR)
-            halo_take(DIR, x_ref)
-        localize()
+            for stage in range(1, HALO + 1):
+                halo_take(DIR, stage, x_ref)
+                localize_stage(l0_ref, stage)
+                if stage == 3:
+                    tile_wait(IDS)
+                    ms_ref[IDS, 0] = tile_table(IDS)
+                    mem_start(IDS, False)
+            build_one_hots()
 
         def partial(r, _):
             total = zero_tile
             for g in range(GROUPS):
                 at = row_tile(r + HALO, g)
-                total = total + em_ref[at, :] * x_ref[at, :].astype(BF16).astype(F32)
+                field = l0_ref[at, :]
+                if iteration:
+                    field = lr_ref[at, :] - first_step * z_ref[at, :] + beta * field
+                total = total + em_ref[at, :] * field.astype(BF16).astype(F32)
             total = total + pltpu.roll(total, 4, 0)
             high, low = split(total)
             adj_ref[pl.ds(pl.multiple_of(r * 8, 8), 8), :] = jnp.where(low_half, high, low)
@@ -441,6 +603,22 @@
         lax.fori_loop(0, NM, gather, 0)
         ms_ref[PICK] = pk_ref[...].T.reshape(NM, NT, 128)
         mem_start(PICK, True)
+        if iteration == 0:
+            x_ref[pl.ds(OWN, ROWS * PAD), :] = lr_ref[pl.ds(OWN, ROWS * PAD), :]
+            for dist in range(1, HALO + 1):
+                halo_take(RES, dist, x_ref)
+            localize_pass(lr_ref, 0)
+        else:
+
+            def turn(r, _):
+                for g in range(GROUPS):
+                    at = row_tile(r + HALO, g)
+                    res = r_ref[at, :] - first_step * im_ref[at, :]
+                    r_ref[at, :] = res
+                    d_ref[at, :] = res + beta * d_ref[at, :]
+                return 0
+
+            lax.fori_loop(0, ROWS, turn, 0)
         mem_wait(PICK)
         summed = mr_ref[PICK, 0]
         for k in range(1, NM):
@@ -448,14 +626,11 @@
         tile_rows(PICK, summed * weight)
         tile_start(PICK, True)
         if iteration == 0:
-            def mask_residual(r, _):
-                sea_row = s_ref[pl.ds(pl.multiple_of(r * 8, 8), 8), :]
-                for g in range(GROUPS):
-                    at = row_tile(r + HALO, g)
-                    y_ref[at, :] = r_ref[at, :] * sea_row
-                return 0
-
-            lax.fori_loop(0, ROWS, mask_residual, 0)
+            localize_pass(lr_ref, 1)
+        else:
+            loaded("sol")
+            for p in range(PLANES):
+                out_sol[p] = sol_ref[p] + first_step * dir_ref[p]
         tile_wait(PICK)
 
         high, low = split(tile_table(PICK))
@@ -477,10 +652,12 @@
         tile_rows(WGT, table[:NT] + table[NT:])
         tile_start(WGT, True)
         if iteration == 0:
-            halo_send(y_ref, RES)
+            localize_pass(lr_ref, 2)
         tile_wait(WGT)
         ms_ref[WGT, 0] = tile_table(WGT)
         mem_start(WGT, False)
+        if iteration == 0:
+            localize_pass(lr_ref, 3)
         mem_wait(WGT)
         pk_ref[...] = mr_ref[WGT].reshape(DEVS, DEVS).T
 
@@ -519,22 +696,27 @@
             tile = (tile + pltpu.roll(tile, 4, 0)) * weight
             ax_ref[pl.ds((HALO + i) * 8, 8), :] = tile
         for side in range(2):
+            tiles = []
             for i in range(HALO // 2):
                 first = HALO + HALO * side + 2 * i
-                as_ref[iteration, side, pl.ds(i * 8, 8), :] = jnp.where(
-                    low_half,
-                    ax_ref[pl.ds(first * 8, 8), :],
-                    ax_ref[pl.ds((first + 1) * 8, 8), :],
+                tiles.append(
+                    jnp.where(
+                        low_half,
+                        ax_ref[pl.ds(first * 8, 8), :],
+                        ax_ref[pl.ds((first + 1) * 8, 8), :],
+                    )
                 )
+            as_ref[iteration, side] = jnp.concatenate(tiles, axis=0).astype(BF16)
         sides_start(*edges, iteration)
         if iteration == 0:
-            sides_wait(*halos, ENS)
-            halo_take(ENS, em_ref)
+            for dist in range(1, HALO + 1):
+                halo_take(ENS, dist, em_ref)
         sides_wait(*edges, iteration)
         for side in range(2):
+            arrived = ar_ref[iteration, side].astype(F32)
             for i in range(HALO // 2):
                 first = (HALO + ROWS) * side + 2 * i
-                packed = ar_ref[iteration, side, pl.ds(i * 8, 8), :]
+                packed = arrived[i * 8 : (i + 1) * 8, :]
                 turned = pltpu.roll(packed, 4, 0)
                 ax_ref[pl.ds(first * 8, 8), :] = jnp.where(low_half, packed, turned)
                 ax_ref[pl.ds((first + 1) * 8, 8), :] = jnp.where(low_half, turned, packed)
@@ -547,7 +729,7 @@
             return 0
 
         lax.fori_loop(0, EXT, back, 0)
-        localize()
+        localize(z_ref)
 
         def image(r, carry):
             sea_row = s_ref[pl.ds(pl.multiple_of(r * 8, 8), 8), :]
@@ -555,11 +737,11 @@
             for g in range(GROUPS):
                 at = row_tile(r + HALO, g)
                 d, res = d_ref[at, :], r_ref[at, :]
-                moved = sea_row * x_ref[at, :]
+                moved = sea_row * z_ref[at, :]
                 img = d + moved
                 im_ref[at, :] = img
                 if iteration == 0:
-                    y_ref[at, :] = img * sea_row
+                    x_ref[at, :] = img * sea_row
                 terms = [d * img, res * res]
                 if iteration == 0:
                     terms += [res * img, img * img]
@@ -571,21 +753,38 @@
         packed = jnp.zeros((8, 128), F32)
         for i, total in enumerate(sums):
             packed = jnp.where(sub_small == i, jnp.sum(total, axis=0, keepdims=True), packed)
-        ms_ref[SUM, 0, pl.ds(0, 8), :] = packed
-        ms_ref[SUM, 0, pl.ds(8, 8), :] = packed
+        ts_ref[SUM, 0] = packed
+        tile_start(SUM, False)
+        if iteration == 0:
+            for dist in range(1, HALO + 1):
+                halo_send(IMG, dist, masked(x_ref))
+            halo_take(IMG, 1, x_ref)
+            localize_stage(z_ref, 1)
+        else:
+            for g in range(GROUPS):
+                d = planes_first(d_ref, g)
+                res = planes_first(r_ref, g)
+                img = planes_first(im_ref, g)
+                for i in range(min(8, PLANES - 8 * g)):
+                    p = 8 * g + i
+                    dir_ref[p] = d[i]
+                    out_res[p] = res[i]
+                    res_ref[p] = img[i]
+        tile_wait(SUM)
+        part = tr_ref[SUM, 0]
+        for k in range(1, NT):
+            part = part + tr_ref[SUM, k]
+        ms_ref[SUM, 0, pl.ds(0, 8), :] = part
+        ms_ref[SUM, 0, pl.ds(8, 8), :] = part
         mem_start(SUM, False)
         if iteration == 0:
-            halo_send(y_ref, IMG)
+            for stage in range(2, HALO + 1):
+                halo_take(IMG, stage, x_ref)
+                localize_stage(z_ref, stage)
         mem_wait(SUM)
-        part = mr_ref[SUM, 0, pl.ds(0, 8), :]
+        total = mr_ref[SUM, 0, pl.ds(0, 8), :]
         for k in range(1, NM):
-            part = part + mr_ref[SUM, k, pl.ds(0, 8), :]
-        ts_ref[SUM, 0] = part
-        tile_start(SUM, False)
-        tile_wait(SUM)
-        total = tr_ref[SUM, 0]
-        for k in range(1, NT):
-            total = total + tr_ref[SUM, k]
+            total = total + mr_ref[SUM, k, pl.ds(0, 8), :]
         total = jnp.sum(total, axis=1, keepdims=True)
         d_image, rr = total[0:1, :], total[1:2, :]
         step = rr / d_image
@@ -594,50 +793,21 @@
             fresh = rr - 2.0 * step * r_image + step * step * image_image
             beta = fresh / rr
             first_step = step
+        else:
             for p in range(PLANES):
-                out_sol[p] = sol_ref[p] + step * dir_ref[p]
-            sides_wait(*halos, RES)
-            sides_wait(*halos, IMG)
-            for side in range(2):
-                for i in range(HALO):
-                    inner = pl.ds(i * PAD, PAD)
-                    outer = pl.ds(side * (OWN + ROWS * PAD) + i * PAD, PAD)
-                    mixed = (
-                        hr_ref[RES, side, inner, :].astype(F32)
-                        - step * hr_ref[IMG, side, inner, :].astype(F32)
-                        + beta * hr_ref[DIR, side, inner, :].astype(F32)
-                    )
-                    x_ref[outer, :] = mixed
-
-            def turn(r, _):
-                sea_row = s_ref[pl.ds(pl.multiple_of(r * 8, 8), 8), :]
-                for g in range(GROUPS):
-                    at = row_tile(r + HALO, g)
-                    res = r_ref[at, :] - step * im_ref[at, :]
-                    r_ref[at, :] = res
-                    fresh_dir = res + beta * d_ref[at, :]
-                    d_ref[at, :] = fresh_dir
-                    x_ref[at, :] = fresh_dir * sea_row
-                return 0
-
-            lax.fori_loop(0, ROWS, turn, 0)
-        else:
-
-            for g in range(GROUPS):
-                d = planes_first(d_ref, g)
-                res = planes_first(r_ref, g)
-                img = planes_first(im_ref, g)
-                for i in range(min(8, PLANES - 8 * g)):
-                    p = 8 * g + i
-                    out_sol[p] = out_sol[p] + step * d[i]
-                    out_res[p] = res[i] - step * img[i]
+                out_sol[p] = out_sol[p] + step * dir_ref[p]
+                out_res[p] = out_res[p] - step * res_ref[p]
 
     for i in range(1 + 3 * ITERS):
         ref = mr_ref.at[i, pl.ds(0, NM - 1)]
         pltpu.make_async_copy(ref, ref, m_send.at[i]).wait()
         ref = tr_ref.at[i, pl.ds(0, NT - 1)]
         pltpu.make_async_copy(ref, ref, t_send.at[i]).wait()
-    for group, many in ((halos, 4), (edges, ITERS), (faces, 1)):
+    for kind in range(4):
+        for dist in range(1, HALO + 1):
+            for copy in halo_piece(kind, dist):
+                copy.wait_send()
+    for group, many in ((edges, ITERS), (faces, 1)):
         for i in range(many):
             for copy in sides(*group, i):
                 copy.wait_send()
@@ -661,35 +831,56 @@
     def planes(x):
         return x.reshape(PLANES, ROWS, LONS)
 
-    row, col = obs_cell // BLOCK, obs_cell % BLOCK
-    key = row * FIELDS + obs_variable * LEVELS + obs_level
-    meta = jnp.stack(
-        [obs_owner[:, 0].astype(F32), col.astype(F32), key.astype(F32), obs_error], axis=0
-    )
+    def row(x):
+        return x.reshape(1, SEGMENT)
+
     exchanges = 1 + 3 * ITERS
     vmem = pl.BlockSpec(memory_space=pltpu.VMEM)
+    hbm = pl.BlockSpec(memory_space=pltpu.HBM)
+    planes_f32 = pltpu.VMEM((PLANES, ROWS, LONS), F32)
+    row_i32 = pltpu.VMEM((1, SEGMENT), jnp.int32)
     field = pltpu.VMEM((EXT * PAD, WIDE), F32)
     band = pltpu.VMEM((EXT * 8, WIDE), F32)
     shape = jax.ShapeDtypeStruct((PLANES, ROWS, LONS), F32)
     sol, res = pl.pallas_call(
         body,
         out_shape=(shape, shape),
-        in_specs=[vmem] * 7 + [pl.BlockSpec(memory_space=pltpu.SMEM), vmem],
+        in_specs=[hbm] * 7 + [pl.BlockSpec(memory_space=pltpu.SMEM)] + [hbm] * 5,
         out_specs=(vmem, vmem),
         scratch_shapes=[
-            field,
-            field,
-            field,
-            field,
-            field,
-            field,
+            planes_f32,
+            planes_f32,
+            planes_f32,
+            pltpu.VMEM((PLANES, ROWS, LONS), BF16),
+            pltpu.VMEM((ROWS, LONS), F32),
+            pltpu.VMEM((ROWS, LONS), F32),
+            pltpu.VMEM((ROWS, LONS), jnp.int32),
+            row_i32,
+            row_i32,
+            row_i32,
+            row_i32,
+            pltpu.VMEM((1, SEGMENT), F32),
+            pltpu.SemaphoreType.DMA((12,)),
+            field,
+            field,
+            field,
+            field,
+            field,
+            field,
+            field,
+            field,
+            field,
+            field,
+            field,
+            band,
+            band,
             band,
             band,
             pltpu.VMEM((ROWS * 8, WIDE), F32),
             pltpu.VMEM((NM, 64, 256), BF16),
             pltpu.VMEM((NM, 256, SLOTS * 128), BF16),
             pltpu.VMEM((DEVS, 128), jnp.int32),
-            pltpu.VMEM((DEVS, 128), jnp.int32),
+            pltpu.VMEM((DEVS, 128), F32),
             pltpu.VMEM((DEVS, 128), F32),
             pltpu.VMEM((NM, 64, 256), F32),
             pltpu.VMEM((64, WIDE), F32),
@@ -697,18 +888,18 @@
             pltpu.VMEM((DEVS, SEGMENT), BF16),
             pltpu.VMEM((2 * NT, SEGMENT), F32),
             pltpu.VMEM((PASSES, 8, 128), F32),
-            pltpu.VMEM((4, 2, EDGE, WIDE), BF16),
-            pltpu.VMEM((4, 2, EDGE, WIDE), BF16),
-            pltpu.VMEM((ITERS, 2, 16, WIDE), F32),
-            pltpu.VMEM((ITERS, 2, 16, WIDE), F32),
+            pltpu.VMEM((4, 2, HALO, PAD, WIDE), BF16),
+            pltpu.VMEM((4, 2, HALO, PAD, WIDE), BF16),
+            pltpu.VMEM((ITERS, 2, 16, WIDE), BF16),
+            pltpu.VMEM((ITERS, 2, 16, WIDE), BF16),
             pltpu.VMEM((1, 2, 8, WIDE), F32),
             pltpu.VMEM((1, 2, 8, WIDE), F32),
             pltpu.VMEM((exchanges, NM, NT, 128), F32),
             pltpu.VMEM((exchanges, NM, NT, 128), F32),
             pltpu.VMEM((exchanges, NT, 8, 128), F32),
             pltpu.VMEM((exchanges, NT, 8, 128), F32),
-            pltpu.SemaphoreType.DMA((4, 2)),
-            pltpu.SemaphoreType.DMA((4, 2)),
+            pltpu.SemaphoreType.DMA((4, HALO, 2)),
+            pltpu.SemaphoreType.DMA((4, HALO, 2)),
             pltpu.SemaphoreType.DMA((ITERS, 2)),
             pltpu.SemaphoreType.DMA((ITERS, 2)),
             pltpu.SemaphoreType.DMA((1, 2)),
@@ -719,7 +910,7 @@
             pltpu.SemaphoreType.DMA((exchanges,)),
         ],
         compiler_params=pltpu.CompilerParams(
-            collective_id=0, has_side_effects=True, vmem_limit_bytes=60 * 1024 * 1024
+            collective_id=0, has_side_effects=True, vmem_limit_bytes=LIMIT
         ),
     )(
         planes(direction),
@@ -730,7 +921,11 @@
         north_rate,
         sea_mask,
         pass_counts,
-        meta,
+        row(obs_owner),
+        row(obs_cell),
+        row(obs_level),
+        row(obs_variable),
+        row(obs_error),
     )
     return sol.reshape(solution.shape), res.reshape(solution.shape)
 

time: 147 us -> 124 us (0.84)
  Pallas kernels: 140 us -> 120 us
  local copies, waits for them, and re-layouts: 5.31 us -> 3.26 us
    pallas_call x1, Pallas kernels: 140 us -> 120 us  [shards(): pl.pallas_call(body, out_shape=(shape, shape), in_specs=[hbm] * 7 + [pl.B...]
    unnamed x14 -> x4, local copies, waits for them, and re-layouts: 5.31 us -> 3.26 us
where the time goes in v2:
time: 124 us
  Pallas kernels  120 us (97%)
  local copies, waits for them, and re-layouts  3.26 us (3%)
    pallas_call x1, Pallas kernels, shards(): pl.pallas_call(body, out_shape=(shape, shape), in_specs=[hbm] * 7 + [pl.B...  120 us
    unnamed x4, local copies, waits for them, and re-layouts  3.26 us

profile of v2, /device:TPU:1, one launch (start us, length us, event | category | flops | bytes accessed | tf_op | source)
XLA Modules:
  0.0 124.1 jit_solution(4670932239665139005)
XLA Ops:
  0.6 120.2 %shard_map.140 = (f32[20,8,1440]{2,1,0:T(8,128)}, f32[20,8,1440]{2,1,0:T(8,128)}) custom-call(f32[20,8,1440]{2,1,0:T(8,128)} %bitcast.11, f32[20,8,1440]{2,1,0:T(8,128)} %bitcast.12, f32[20,8,1440]{2,1,0:T(8,128)} %bitcast.13, bf16[20,8,1440]{2,1,0:T(8,128)(2,1)} %bitcast.16, f32[8,1440]{1,0:T(8,128)} %east_hbm.1, f32[8,1440]{1,0:T(8,128)} %north_hbm.1, ...), custom_call_target="tpu_custom_call" | custom-call | tf_op jit(solution)/shard_map/pallas_call | solution.py:845
  120.8 0.0 copy-start
  120.8 2.3 %copy.17 = f32[5,4,8,1440]{3,2,1,0:T(8,128)} copy(f32[5,4,8,1440]{3,2,1,0:T(8,128)} %bitcast.15) | data formatting | bytes 1843200
  123.2 0.0 copy-done
  123.2 0.9 copy.18
Async XLA Ops:
  120.8 2.3 %copy-start = (f32[20,8,1440]{2,1,0:T(8,128)S(1)}, f32[20,8,1440]{2,1,0:T(8,128)}, u32[]{:S(2)}) copy-start(f32[20,8,1440]{2,1,0:T(8,128)} %get-tuple-element.5) | copy-start | bytes 2764804

commit v3 on v2

--- a/solution.py
+++ b/solution.py
@@ -401,10 +401,10 @@
 
     def tile_rows(i, table):
         for k in range(NT):
-            ts_ref[i, k] = jnp.broadcast_to(table[k : k + 1, :], (8, 128))
+            ts_ref[i, k] = table[k : k + 1, :]
 
     def tile_table(i):
-        return tr_ref[i][:, 0, :]
+        return jnp.concatenate([tr_ref[i, k] for k in range(NT)], axis=0)
 
     table = to_table(col_id, rf_id)
     tile_rows(IDS, table[NT:] * 256.0 + table[:NT])
@@ -427,8 +427,6 @@
         turned = rows_first(ens_ref, g)
         for i in range(ROWS):
             em_ref[row_tile(HALO + i, g), :] = turned[i] * sea_rows(i)
-    for dist in range(1, HALO + 1):
-        halo_send(ENS, dist, masked(em_ref))
 
     sides_wait(*faces, 0)
     below, above = cr_ref[0, 0], cr_ref[0, 1]
@@ -457,7 +455,7 @@
     levels = (x_ref, p1_ref, p2_ref, p3_ref)
 
     def localization(result):
-        def passing(k, first, second):
+        def passing(k, *rows):
             src = levels[k]
             dst = levels[k + 1] if k + 1 < PASSES else result
             keep = jnp.broadcast_to(pass_ref[k][:, 0:1], (8, 128)) > 0.0
@@ -495,15 +493,18 @@
                         dst[at, cols] = jnp.where(keep, total, v)
                         near[g], last[g] = following, west
 
-            row(first)
-            row(second)
+            for r in rows:
+                row(r)
 
         def across(k, low, high):
-            def pair(i, _):
-                passing(k, low + 2 * i, low + 2 * i + 1)
+            def quad(i, _):
+                passing(k, *(low + 4 * i + j for j in range(4)))
                 return 0
 
-            lax.fori_loop(0, (high - low) // 2, pair, 0)
+            whole = (high - low) // 4
+            lax.fori_loop(0, whole, quad, 0)
+            if low + 4 * whole < high:
+                passing(k, *range(low + 4 * whole, high))
 
         return passing, across
 
@@ -552,6 +553,36 @@
         start = BLOCK * b
         first = (start // 128) * 128
         return first, start - first
+
+    segment = lax.broadcasted_iota(jnp.int32, (1, 128), 1) // 32
+
+    def sums_start(i, totals):
+        packed = jnp.zeros((1, 128), F32)
+        for k, total in enumerate(totals):
+            total = jnp.sum(total, axis=0, keepdims=True)
+            total = total + pltpu.roll(total, 64, 1)
+            total = total + pltpu.roll(total, 32, 1)
+            packed = jnp.where(segment == k, total, packed)
+        ts_ref[i, 0] = packed
+        tile_start(i, False)
+
+    def sums_pass_on(i):
+        tile_wait(i)
+        part = tr_ref[i, 0]
+        for k in range(1, NT):
+            part = part + tr_ref[i, k]
+        ms_ref[i, 0] = jnp.broadcast_to(part, (NT, 128))
+        mem_start(i, False)
+
+    def sums_get(i):
+        mem_wait(i)
+        total = mr_ref[i, 0, pl.ds(0, 8), :]
+        for k in range(1, NM):
+            total = total + mr_ref[i, k, pl.ds(0, 8), :]
+        total = total[0:1, :]
+        return [
+            jnp.sum(jnp.where(segment == k, total, 0.0), axis=1, keepdims=True) for k in range(4)
+        ]
 
     for iteration in range(ITERS):
         base = 1 + 3 * iteration
@@ -600,7 +631,7 @@
             pk_ref[rows16, :] = jnp.concatenate(rows, axis=0)
             return 0
 
-        lax.fori_loop(0, NM, gather, 0)
+        lax.fori_loop(0, NM, gather, 0, unroll=2)
         ms_ref[PICK] = pk_ref[...].T.reshape(NM, NT, 128)
         mem_start(PICK, True)
         if iteration == 0:
@@ -610,15 +641,18 @@
             localize_pass(lr_ref, 0)
         else:
 
-            def turn(r, _):
+            def turn(r, carry):
+                rr, dd = carry
                 for g in range(GROUPS):
                     at = row_tile(r + HALO, g)
                     res = r_ref[at, :] - first_step * im_ref[at, :]
+                    d = res + beta * d_ref[at, :]
                     r_ref[at, :] = res
-                    d_ref[at, :] = res + beta * d_ref[at, :]
-                return 0
-
-            lax.fori_loop(0, ROWS, turn, 0)
+                    d_ref[at, :] = d
+                    rr, dd = rr + fold(res * res, valid), dd + fold(d * d, valid)
+                return rr, dd
+
+            own_rr, own_dd = lax.fori_loop(0, ROWS, turn, (jnp.zeros((8, 128), F32),) * 2)
         mem_wait(PICK)
         summed = mr_ref[PICK, 0]
         for k in range(1, NM):
@@ -626,6 +660,8 @@
         tile_rows(PICK, summed * weight)
         tile_start(PICK, True)
         if iteration == 0:
+            halo_send(ENS, 1, masked(em_ref))
+            halo_send(ENS, 2, masked(em_ref))
             localize_pass(lr_ref, 1)
         else:
             loaded("sol")
@@ -652,12 +688,23 @@
         tile_rows(WGT, table[:NT] + table[NT:])
         tile_start(WGT, True)
         if iteration == 0:
+            halo_send(ENS, 3, masked(em_ref))
+            halo_send(ENS, 4, masked(em_ref))
+        else:
+            product = value * weighted
+            observed = product[:, 0:128]
+            for k in range(1, SEGMENT // 128):
+                observed = observed + product[:, 128 * k : 128 * (k + 1)]
+            sums_start(SUM, (own_dd, own_rr, observed))
+        if iteration == 0:
             localize_pass(lr_ref, 2)
         tile_wait(WGT)
         ms_ref[WGT, 0] = tile_table(WGT)
         mem_start(WGT, False)
         if iteration == 0:
             localize_pass(lr_ref, 3)
+        else:
+            sums_pass_on(SUM)
         mem_wait(WGT)
         pk_ref[...] = mr_ref[WGT].reshape(DEVS, DEVS).T
 
@@ -677,7 +724,7 @@
             )
             return 0
 
-        lax.fori_loop(0, NM, scatter, 0)
+        lax.fori_loop(0, NM, scatter, 0, unroll=2)
         adj_ref[...] = jnp.zeros((64, WIDE), F32)
         for b in range(NM):
             first, shift = window(b)
@@ -708,9 +755,30 @@
                 )
             as_ref[iteration, side] = jnp.concatenate(tiles, axis=0).astype(BF16)
         sides_start(*edges, iteration)
+        if iteration:
+            d_square, rr, observed, _ = sums_get(SUM)
+            step = rr / (d_square + observed)
+            for g in range(GROUPS):
+                d = planes_first(d_ref, g)
+                for i in range(min(8, PLANES - 8 * g)):
+                    p = 8 * g + i
+                    out_sol[p] = out_sol[p] + step * d[i]
         if iteration == 0:
             for dist in range(1, HALO + 1):
                 halo_take(ENS, dist, em_ref)
+        def back(r, _):
+            row = ax_ref[pl.ds(pl.multiple_of(r * 8, 8), 8), :]
+            for g in range(GROUPS):
+                at = row_tile(r, g)
+                x_ref[at, :] = (em_ref[at, :] * row).astype(BF16).astype(F32)
+            return 0
+
+        passing, _ = localization(z_ref)
+        lax.fori_loop(HALO, HALO + ROWS, back, 0)
+        for k in range(PASSES - 1):
+            inside = list(range(HALO + 1 + k, HALO + ROWS - 1 - k))
+            for first in range(0, len(inside), 4):
+                passing(k, *inside[first : first + 4])
         sides_wait(*edges, iteration)
         for side in range(2):
             arrived = ar_ref[iteration, side].astype(F32)
@@ -721,15 +789,28 @@
                 ax_ref[pl.ds(first * 8, 8), :] = jnp.where(low_half, packed, turned)
                 ax_ref[pl.ds((first + 1) * 8, 8), :] = jnp.where(low_half, turned, packed)
 
-        def back(r, _):
-            row = ax_ref[pl.ds(pl.multiple_of(r * 8, 8), 8), :]
+        lax.fori_loop(0, HALO, back, 0)
+        lax.fori_loop(HALO + ROWS, EXT, back, 0)
+        for k in range(PASSES):
+
+            def outside(i, _):
+                base = 1 + k + (10 - 2 * k) * i
+                passing(k, *(base + j for j in range(4)))
+                return 0
+
+            lax.fori_loop(0, 2, outside, 0)
+
+        if iteration + 1 == ITERS:
             for g in range(GROUPS):
-                at = row_tile(r, g)
-                x_ref[at, :] = (em_ref[at, :] * row).astype(BF16).astype(F32)
-            return 0
-
-        lax.fori_loop(0, EXT, back, 0)
-        localize(z_ref)
+                rows = []
+                for i in range(ROWS):
+                    at = row_tile(HALO + i, g)
+                    image = d_ref[at, :] + sea_rows(i) * z_ref[at, :]
+                    rows.append(r_ref[at, :] - step * image)
+                turned = jnp.stack(rows, axis=0).transpose(1, 0, 2)
+                for i in range(min(8, PLANES - 8 * g)):
+                    out_res[8 * g + i] = turned[i][:, :LONS]
+            continue
 
         def image(r, carry):
             sea_row = s_ref[pl.ds(pl.multiple_of(r * 8, 8), 8), :]
@@ -737,66 +818,26 @@
             for g in range(GROUPS):
                 at = row_tile(r + HALO, g)
                 d, res = d_ref[at, :], r_ref[at, :]
-                moved = sea_row * z_ref[at, :]
-                img = d + moved
+                img = d + sea_row * z_ref[at, :]
                 im_ref[at, :] = img
-                if iteration == 0:
-                    x_ref[at, :] = img * sea_row
-                terms = [d * img, res * res]
-                if iteration == 0:
-                    terms += [res * img, img * img]
+                x_ref[at, :] = img * sea_row
+                terms = (d * img, res * res, res * img, img * img)
                 sums = [total + fold(term, valid) for total, term in zip(sums, terms)]
             return tuple(sums)
 
-        count_sums = 4 if iteration == 0 else 2
-        sums = lax.fori_loop(0, ROWS, image, (jnp.zeros((8, 128), F32),) * count_sums)
-        packed = jnp.zeros((8, 128), F32)
-        for i, total in enumerate(sums):
-            packed = jnp.where(sub_small == i, jnp.sum(total, axis=0, keepdims=True), packed)
-        ts_ref[SUM, 0] = packed
-        tile_start(SUM, False)
-        if iteration == 0:
-            for dist in range(1, HALO + 1):
-                halo_send(IMG, dist, masked(x_ref))
-            halo_take(IMG, 1, x_ref)
-            localize_stage(z_ref, 1)
-        else:
-            for g in range(GROUPS):
-                d = planes_first(d_ref, g)
-                res = planes_first(r_ref, g)
-                img = planes_first(im_ref, g)
-                for i in range(min(8, PLANES - 8 * g)):
-                    p = 8 * g + i
-                    dir_ref[p] = d[i]
-                    out_res[p] = res[i]
-                    res_ref[p] = img[i]
-        tile_wait(SUM)
-        part = tr_ref[SUM, 0]
-        for k in range(1, NT):
-            part = part + tr_ref[SUM, k]
-        ms_ref[SUM, 0, pl.ds(0, 8), :] = part
-        ms_ref[SUM, 0, pl.ds(8, 8), :] = part
-        mem_start(SUM, False)
-        if iteration == 0:
-            for stage in range(2, HALO + 1):
-                halo_take(IMG, stage, x_ref)
-                localize_stage(z_ref, stage)
-        mem_wait(SUM)
-        total = mr_ref[SUM, 0, pl.ds(0, 8), :]
-        for k in range(1, NM):
-            total = total + mr_ref[SUM, k, pl.ds(0, 8), :]
-        total = jnp.sum(total, axis=1, keepdims=True)
-        d_image, rr = total[0:1, :], total[1:2, :]
-        step = rr / d_image
-        if iteration == 0:
-            r_image, image_image = total[2:3, :], total[3:4, :]
-            fresh = rr - 2.0 * step * r_image + step * step * image_image
-            beta = fresh / rr
-            first_step = step
-        else:
-            for p in range(PLANES):
-                out_sol[p] = out_sol[p] + step * dir_ref[p]
-                out_res[p] = out_res[p] - step * res_ref[p]
+        sums_start(SUM, lax.fori_loop(0, ROWS, image, (jnp.zeros((8, 128), F32),) * 4))
+        for dist in range(1, HALO + 1):
+            halo_send(IMG, dist, masked(x_ref))
+        halo_take(IMG, 1, x_ref)
+        localize_stage(z_ref, 1)
+        sums_pass_on(SUM)
+        for stage in range(2, HALO + 1):
+            halo_take(IMG, stage, x_ref)
+            localize_stage(z_ref, stage)
+        d_image, rr, r_image, image_image = sums_get(SUM)
+        first_step = rr / d_image
+        fresh = rr - 2.0 * first_step * r_image + first_step * first_step * image_image
+        beta = fresh / rr
 
     for i in range(1 + 3 * ITERS):
         ref = mr_ref.at[i, pl.ds(0, NM - 1)]
@@ -896,8 +937,8 @@
             pltpu.VMEM((1, 2, 8, WIDE), F32),
             pltpu.VMEM((exchanges, NM, NT, 128), F32),
             pltpu.VMEM((exchanges, NM, NT, 128), F32),
-            pltpu.VMEM((exchanges, NT, 8, 128), F32),
-            pltpu.VMEM((exchanges, NT, 8, 128), F32),
+            pltpu.VMEM((exchanges, NT, 1, 128), F32),
+            pltpu.VMEM((exchanges, NT, 1, 128), F32),
             pltpu.SemaphoreType.DMA((4, HALO, 2)),
             pltpu.SemaphoreType.DMA((4, HALO, 2)),
             pltpu.SemaphoreType.DMA((ITERS, 2)),

time: 124 us -> 106 us (0.85)
  Pallas kernels: 120 us -> 102 us
    pallas_call x1, Pallas kernels: 120 us -> 102 us  [shards(): pl.pallas_call(body, out_shape=(shape, shape), in_specs=[hbm] * 7 + [pl.B...]
where the time goes in v3:
time: 106 us
  Pallas kernels  102 us (96%)
  local copies, waits for them, and re-layouts  3.26 us (3%)
    pallas_call x1, Pallas kernels, shards(): pl.pallas_call(body, out_shape=(shape, shape), in_specs=[hbm] * 7 + [pl.B...  102 us
    unnamed x4, local copies, waits for them, and re-layouts  3.26 us

profile of v3, /device:TPU:1, one launch (start us, length us, event | category | flops | bytes accessed | tf_op | source)
XLA Modules:
  0.0 106.3 jit_solution(14069085854113585523)
XLA Ops:
  0.6 102.4 %shard_map.140 = (f32[20,8,1440]{2,1,0:T(8,128)}, f32[20,8,1440]{2,1,0:T(8,128)}) custom-call(f32[20,8,1440]{2,1,0:T(8,128)} %bitcast.11, f32[20,8,1440]{2,1,0:T(8,128)} %bitcast.12, f32[20,8,1440]{2,1,0:T(8,128)} %bitcast.13, bf16[20,8,1440]{2,1,0:T(8,128)(2,1)} %bitcast.16, f32[8,1440]{1,0:T(8,128)} %east_hbm.1, f32[8,1440]{1,0:T(8,128)} %north_hbm.1, ...), custom_call_target="tpu_custom_call" | custom-call | tf_op jit(solution)/shard_map/pallas_call | solution.py:886
  103.0 0.0 copy-start
  103.1 2.3 %copy.17 = f32[5,4,8,1440]{3,2,1,0:T(8,128)} copy(f32[5,4,8,1440]{3,2,1,0:T(8,128)} %bitcast.15) | data formatting | bytes 1843200
  105.4 0.0 copy-done
  105.4 0.9 copy.18
Async XLA Ops:
  103.0 2.3 %copy-start = (f32[20,8,1440]{2,1,0:T(8,128)S(1)}, f32[20,8,1440]{2,1,0:T(8,128)}, u32[]{:S(2)}) copy-start(f32[20,8,1440]{2,1,0:T(8,128)} %get-tuple-element.5) | copy-start | bytes 2764804

commit v4 on v3

--- a/solution.py
+++ b/solution.py
@@ -366,7 +366,6 @@
         return lambda r: ref[whole_row(r), :]
 
     halo_send(DIR, 1, masked(x_ref))
-    halo_send(DIR, 2, masked(x_ref))
 
     loaded("owner", "cell", "level", "variable", "error")
     owner = owner_ref[...]
@@ -410,6 +409,7 @@
     tile_rows(IDS, table[NT:] * 256.0 + table[:NT])
 
     tile_start(IDS, True)
+    halo_send(DIR, 2, masked(x_ref))
     halo_send(DIR, 3, masked(x_ref))
     halo_send(DIR, 4, masked(x_ref))
 
@@ -591,7 +591,7 @@
             for stage in range(1, HALO + 1):
                 halo_take(DIR, stage, x_ref)
                 localize_stage(l0_ref, stage)
-                if stage == 3:
+                if stage == 2:
                     tile_wait(IDS)
                     ms_ref[IDS, 0] = tile_table(IDS)
                     mem_start(IDS, False)

time: 106 us -> 105 us (level)
    pallas_call x1, Pallas kernels: 102 us -> 101 us  [shards(): pl.pallas_call(body, out_shape=(shape, shape), in_specs=[hbm] * 7 + [pl.B...]
where the time goes in v4:
time: 105 us
  Pallas kernels  101 us (96%)
  local copies, waits for them, and re-layouts  3.26 us (3%)
    pallas_call x1, Pallas kernels, shards(): pl.pallas_call(body, out_shape=(shape, shape), in_specs=[hbm] * 7 + [pl.B...  101 us
    unnamed x4, local copies, waits for them, and re-layouts  3.26 us

profile of v4, /device:TPU:1, one launch (start us, length us, event | category | flops | bytes accessed | tf_op | source)
XLA Modules:
  0.0 104.6 jit_solution(4238395152089190127)
XLA Ops:
  0.6 100.7 %shard_map.140 = (f32[20,8,1440]{2,1,0:T(8,128)}, f32[20,8,1440]{2,1,0:T(8,128)}) custom-call(f32[20,8,1440]{2,1,0:T(8,128)} %bitcast.11, f32[20,8,1440]{2,1,0:T(8,128)} %bitcast.12, f32[20,8,1440]{2,1,0:T(8,128)} %bitcast.13, bf16[20,8,1440]{2,1,0:T(8,128)(2,1)} %bitcast.16, f32[8,1440]{1,0:T(8,128)} %east_hbm.1, f32[8,1440]{1,0:T(8,128)} %north_hbm.1, ...), custom_call_target="tpu_custom_call" | custom-call | tf_op jit(solution)/shard_map/pallas_call | solution.py:886
  101.3 0.0 copy-start
  101.3 2.3 %copy.17 = f32[5,4,8,1440]{3,2,1,0:T(8,128)} copy(f32[5,4,8,1440]{3,2,1,0:T(8,128)} %bitcast.15) | data formatting | bytes 1843200
  103.6 0.0 copy-done
  103.6 0.9 copy.18
Async XLA Ops:
  101.3 2.3 %copy-start = (f32[20,8,1440]{2,1,0:T(8,128)S(1)}, f32[20,8,1440]{2,1,0:T(8,128)}, u32[]{:S(2)}) copy-start(f32[20,8,1440]{2,1,0:T(8,128)} %get-tuple-element.5) | copy-start | bytes 2764804
